TPU v7x, 32 devices: a whole 2x2x4 slice. The times are simulated.
32 devices in a mesh: dp: 8 (over z, x), neg: 4 (over y, core).
Axes of the slice: x: 2, y: 2, z: 4, core: 2. Of those that a mesh axis runs over, the one named last changes fastest.
Arguments:
- history: bfloat16 [6144, 512], P('dp'), may hold values from -6 to 6
- lengths: int32 [16], P('dp'), may hold values from 1 to 384
- w_in: bfloat16 [512, 2048], P(None, 'neg'), may hold values from -0.25 to 0.25
- w_out: bfloat16 [512, 512], P('neg'), may hold values from -0.25 to 0.25
- target_ids: int32 [6144], P('dp'), may hold values from 0 to 8191
- negative_ids: int32 [16384], P('neg'), may hold values from 0 to 8191, as said below
- item_table: bfloat16 [8192, 512], P('neg'), may hold values from -6 to 6
Outputs:
- token_loss: float32 [6144], P('dp')
- grad_w_in: float32 [512, 2048], P('dp', 'neg')
- grad_w_out: float32 [512, 512], P('neg', 'dp')
- grad_table: float32 [8192, 512], P(('neg', 'dp'))
Inputs may be any that keep to these rules, and one draw needn't show every extreme that they name: `negative_ids`: negative n names one of the rows (n // 4096) * 2048 to (n // 4096 + 1) * 2048 - 1.
All inputs are finite; a program needn't handle non-finite values.
Results may differ from a plain program's by a relative error of at most 0.0098.
Values may be sent and summed in bfloat16 or wider, within the bound.
A program may use at most 128 MiB of HBM per device.

v0:
```python
import jax
import jax.numpy as jnp
from jax import lax
from jax.sharding import PartitionSpec as P

HEAD = 64


logit_scale = 64.0
epsilon = 1e-06


def silu_grad(values):
    logistic = jax.nn.sigmoid(values)
    return logistic * (1.0 + values * (1.0 - logistic))


def moment_norm(values):
    row_mean = jnp.mean(values, -1, keepdims=True)
    row_square = jnp.mean(values * values, -1, keepdims=True)
    norm_scale = lax.rsqrt(row_square - row_mean * row_mean + epsilon)
    return ((values - row_mean) * norm_scale, norm_scale)


def normalize_rows(values):
    inverse = lax.rsqrt(jnp.sum(values * values, -1, keepdims=True) + epsilon)
    return (values * inverse, inverse)


def project_rows(raw_rows, unit_part, inverse):
    return (raw_rows - unit_part * jnp.sum(raw_rows * unit_part, -1, keepdims=True)) * inverse


def scatter_sum(values, axis_name):
    pieces = lax.axis_size(axis_name)
    parts = values.astype(jnp.bfloat16).reshape(pieces, values.shape[0] // pieces, values.shape[1])
    received = lax.all_to_all(parts, axis_name, 0, 0)
    return jnp.sum(received.astype(jnp.float32), 0)


def count_rows(slots, row_count):
    lanes = 128
    coarse = (slots // lanes)[None, :] == jnp.arange(row_count // lanes, dtype=jnp.int32)[:, None]
    fine = (slots % lanes)[:, None] == jnp.arange(lanes, dtype=jnp.int32)[None, :]
    table = jnp.dot(
        coarse.astype(jnp.bfloat16), fine.astype(jnp.bfloat16), preferred_element_type=jnp.float32
    )
    return table.reshape(1, row_count)


def on_device(history, lengths, w_in, w_out, target_ids, negative_ids, item_table):
    tok_rows, model_width = history.shape
    user_count = lengths.shape[0]
    hist_len = tok_rows // user_count
    local_heads = w_in.shape[1] // (4 * HEAD)
    local_width = local_heads * HEAD
    item_rows = item_table.shape[0]
    groups = lax.axis_size("neg")
    share_rows = tok_rows // groups
    share_start = lax.axis_index("neg") * share_rows
    item_base = lax.axis_index("neg") * item_rows
    inputs_float = history.astype(jnp.float32)
    normed = moment_norm(inputs_float)[0].astype(jnp.bfloat16)
    pre_act = jnp.dot(normed, w_in, preferred_element_type=jnp.float32)
    projected = (
        jax.nn.silu(pre_act)
        .astype(jnp.bfloat16)
        .reshape(user_count, hist_len, local_heads, 4, HEAD)
    )
    gate_rows = projected[:, :, :, 0]
    value_rows = projected[:, :, :, 1]
    query_rows = projected[:, :, :, 2]
    key_rows = projected[:, :, :, 3]
    scores = jnp.einsum("bihd,bjhd->bhij", query_rows, key_rows, preferred_element_type=jnp.float32)
    position = jnp.arange(hist_len, dtype=jnp.int32)
    live_slots = position[None, :] < lengths[:, None]
    causal = position[None, :] <= position[:, None]
    attn_mask = (causal[None] & live_slots[:, :, None]).astype(jnp.float32)[:, None]
    attn_weights = (jax.nn.silu(scores) * attn_mask / hist_len).astype(jnp.bfloat16)
    attended = jnp.einsum(
        "bhij,bjhd->bihd", attn_weights, value_rows, preferred_element_type=jnp.float32
    ).reshape(tok_rows, local_width)
    head_sums = lax.psum((jnp.sum(attended, -1), jnp.sum(attended * attended, -1)), "neg")
    row_mean = head_sums[0][:, None] / model_width
    norm_scale = lax.rsqrt(head_sums[1][:, None] / model_width - row_mean * row_mean + epsilon)
    centred = (attended - row_mean) * norm_scale
    gate_flat = gate_rows.reshape(tok_rows, local_width).astype(jnp.float32)
    mixed_rows = (centred * gate_flat).astype(jnp.bfloat16)
    branch = jnp.dot(mixed_rows, w_out, preferred_element_type=jnp.float32)
    branch_part = scatter_sum(branch, "neg")
    inputs_part = lax.dynamic_slice_in_dim(inputs_float, share_start, share_rows, 0)
    user_unit, user_inverse = normalize_rows(inputs_part + branch_part)
    user_rounded = lax.all_gather(user_unit.astype(jnp.bfloat16), "neg", axis=0, tiled=True)
    item_unit, item_inverse = normalize_rows(item_table.astype(jnp.float32))
    item_rounded = item_unit.astype(jnp.bfloat16)
    row_counts = count_rows(negative_ids - item_base, item_rows)
    is_target = (target_ids - item_base)[:, None] == jnp.arange(item_rows, dtype=jnp.int32)[None, :]
    logits = logit_scale * lax.dot_general(
        user_rounded, item_rounded, (((1,), (1,)), ((), ())), preferred_element_type=jnp.float32
    )
    exp_terms = jnp.where(is_target, 0.0, row_counts * jnp.exp(logits))
    positive, negative_sum = lax.psum(
        (jnp.sum(jnp.where(is_target, logits, 0.0), -1), jnp.sum(exp_terms, -1)), "neg"
    )
    partition_sum = jnp.exp(positive) + negative_sum
    live_rows = live_slots.reshape(tok_rows).astype(jnp.float32)
    token_loss = live_rows * (jnp.log(partition_sum) - positive)
    positive_grad = live_rows * (jnp.exp(positive) / partition_sum - 1.0)
    row_factor = live_rows / partition_sum
    coefficients = jnp.where(
        is_target, positive_grad[:, None], row_factor[:, None] * exp_terms
    ).astype(jnp.bfloat16)
    unit_part = logit_scale * jnp.dot(
        coefficients, item_rounded, preferred_element_type=jnp.float32
    )
    row_raw = logit_scale * lax.dot_general(
        coefficients, user_rounded, (((0,), (0,)), ((), ())), preferred_element_type=jnp.float32
    )
    row_total = scatter_sum(row_raw, "dp")
    unit_grad = scatter_sum(unit_part, "neg")
    output_part = project_rows(unit_grad, user_unit, user_inverse).astype(jnp.bfloat16)
    output_rounded = lax.all_gather(output_part, "neg", axis=0, tiled=True)
    grad_out_local = lax.dot_general(
        output_rounded, mixed_rows, (((0,), (0,)), ((), ())), preferred_element_type=jnp.float32
    )
    mixed_grad = lax.dot_general(
        output_rounded, w_out, (((1,), (1,)), ((), ())), preferred_element_type=jnp.float32
    )
    centred_grad = mixed_grad * gate_flat
    gate_grad = mixed_grad * centred
    back_sums = lax.psum((jnp.sum(centred_grad, -1), jnp.sum(centred_grad * centred, -1)), "neg")
    attended_grad = norm_scale * (
        centred_grad
        - back_sums[0][:, None] / model_width
        - centred * back_sums[1][:, None] / model_width
    )
    attended_grad = attended_grad.astype(jnp.bfloat16).reshape(
        user_count, hist_len, local_heads, HEAD
    )
    weight_grad = jnp.einsum(
        "bihd,bjhd->bhij", attended_grad, value_rows, preferred_element_type=jnp.float32
    )
    value_grad = jnp.einsum(
        "bhij,bihd->bjhd", attn_weights, attended_grad, preferred_element_type=jnp.float32
    )
    score_grad = (weight_grad * attn_mask / hist_len * silu_grad(scores)).astype(jnp.bfloat16)
    query_grad = jnp.einsum(
        "bhij,bjhd->bihd", score_grad, key_rows, preferred_element_type=jnp.float32
    )
    key_grad = jnp.einsum(
        "bhij,bihd->bjhd", score_grad, query_rows, preferred_element_type=jnp.float32
    )
    project_grad = jnp.stack(
        [
            gate_grad.reshape(user_count, hist_len, local_heads, HEAD),
            value_grad,
            query_grad,
            key_grad,
        ],
        3,
    ).reshape(tok_rows, 4 * local_width)
    pre_grad = (project_grad * silu_grad(pre_act)).astype(jnp.bfloat16)
    grad_in_local = lax.dot_general(
        normed, pre_grad, (((0,), (0,)), ((), ())), preferred_element_type=jnp.float32
    )
    grad_w_in = scatter_sum(grad_in_local, "dp")
    grad_w_out = (
        scatter_sum(grad_out_local, "dp")
        .T
    )
    table_share = item_rows // lax.axis_size("dp")
    own_first = lax.axis_index("dp") * table_share
    grad_table = project_rows(
        row_total,
        lax.dynamic_slice_in_dim(item_unit, own_first, table_share, 0),
        lax.dynamic_slice_in_dim(item_inverse, own_first, table_share, 0),
    )
    return (token_loss, grad_w_in, grad_w_out, grad_table)


def solution(mesh):
    placed = (
        P("dp", None),
        P("dp"),
        P(None, "neg"),
        P("neg", None),
        P("dp"),
        P("neg"),
        P("neg", None),
    )
    return jax.shard_map(
        on_device,
        mesh=mesh,
        in_specs=placed,
        out_specs=(P("dp"), P("dp", "neg"), P("neg", "dp"), P(("neg", "dp"), None)),
        check_vma=False,
    )
```

profile of v0, /device:TPU:0, one launch (start us, length us, event | category | flops | bytes accessed | tf_op | source)
XLA Modules:
  0.0 199.1 jit_solution(16149818400746306628)
XLA Ops:
  0.7 0.8 iota_compare_fusion.8
  1.5 1.4 convert_reduce_fusion.3
  2.9 3.1 %multiply_convert_fusion.5 = (bf16[768,512]{1,0:T(8,128)(2,1)S(1)}, f32[768,512]{1,0:T(8,128)}) fusion(bf16[512,512]{1,0:T(8,128)(2,1)S(1)} %copy-done, bf16[768,512]{1,0:T(8,128)(2,1)} %param.7, f32[768]{0:T(1024)S(1)} %get-tuple-element.33, f32[768]{0:T(1024)S(1)} %get-tuple-element.32), kind=kOutput, calls=%fused_computation.20 | convolution fusion | flops 406192128 | bytes 3676160 | tf_op jit(solution)/shard_map/dot_general | solution.py:64
  6.5 0.5 fusion.19
  7.3 2.2 %multiply_convert_fusion.2 = (bf16[2,2,384,384]{3,2,1,0:T(8,128)(2,1)S(1)}, f32[2,2,384,384]{3,2,1,0:T(8,128)}) fusion(f32[2,384,384]{2,1,0:T(8,128)S(1)} %and_convert_fusion, bf16[2,384,2,1,64]{1,0,4,3,2:T(2,128)(2,1)S(1)} %get-tuple-element.25, bf16[2,384,2,1,64]{1,0,4,3,2:T(2,128)(2,1)S(1)} %get-tuple-element.23), kind=kOutput, calls=%fused_computation.11 | convolution fusion | flops 79626240 | bytes 5111808 | tf_op jit(solution)/shard_map/bihd,bjhd->bhij/dot_general | solution.py:74
  9.6 0.6 fusion.18
  10.6 8.5 %all-reduce.2 = (f32[768]{0:T(1024)S(1)}, f32[768]{0:T(1024)S(1)}) all-reduce(f32[768]{0:T(1024)S(1)} %reduce_sum.162, f32[768]{0:T(1024)S(1)} %reduce_sum.160), channel_id=1, replica_groups=mesh['dp'=8,'neg'=4] {'neg'}, use_global_device_ids=true, to_apply=%region_5.6 | all-reduce | flops 1536 | bytes 12288 | tf_op jit(solution)/shard_map/psum | solution.py:83
  19.3 1.3 convolution_convert_fusion
  20.6 4.3 %all-to-all-start = ((bf16[4,192,512]{2,1,0:T(8,128)(2,1)}), bf16[4,192,512]{2,1,0:T(8,128)(2,1)}, u32[]{:S(2)}, u32[]{:S(2)}) async-start(bf16[4,192,512]{2,1,0:T(8,128)(2,1)} %bitcast.76), calls=%async_computation | async-start | bytes 1572864 | tf_op jit(solution)/shard_map/all_to_all | solution.py:37
  25.5 2.5 %convert_element_type.87 = f32[768,512]{1,0:T(8,128)} convert(bf16[768,512]{1,0:T(8,128)(2,1)} %param.7) | non-fusion elementwise | flops 393216 | bytes 2359296 | tf_op jit(solution)/shard_map/convert_element_type | solution.py:62
  28.0 0.6 broadcast_subtract_fusion
  28.6 1.3 fusion.3
  30.4 6.2 %all-to-all-done = bf16[4,192,512]{2,1,0:T(8,128)(2,1)} async-done(((bf16[4,192,512]{2,1,0:T(8,128)(2,1)}), bf16[4,192,512]{2,1,0:T(8,128)(2,1)}, u32[]{:S(2)}, u32[]{:S(2)}) %all-to-all-start) | async-done | bytes 786464 | tf_op jit(solution)/shard_map/all_to_all | solution.py:37
  36.6 1.3 convert_reduce_fusion.2
  37.9 1.1 multiply_reduce_fusion.4
  39.0 0.6 copy-done.24
  39.7 7.9 %all_gather.6 = bf16[768,512]{1,0:T(8,128)(2,1)S(1)} all-gather(bf16[192,512]{1,0:T(8,128)(2,1)S(1)} %multiply_convert_fusion.11), channel_id=1, replica_groups=mesh['dp'=8,'neg'=4] {'neg'}, dimensions={0}, use_global_device_ids=true | all-gather | bytes 983040 | tf_op jit(solution)/shard_map/all_gather | solution.py:93
  47.6 6.5 %fusion = (f32[768]{0:T(1024)}, f32[768]{0:T(1024)}, f32[768,2048]{1,0:T(8,128)}) fusion(f32[2048]{0:T(1024)} %fusion.3, s32[768]{0:T(1024)} %broadcast_subtract_fusion, bf16[768,512]{1,0:T(8,128)(2,1)S(1)} %all_gather.6, f32[2048]{0:T(1024)S(1)} %add_rsqrt_fusion, bf16[2048,512]{1,0:T(8,128)(2,1)S(1)} %copy-done.1), kind=kOutput, calls=%fused_computation.6 | convolution fusion | flops 1624766976 | bytes 9200640 | tf_op jit(solution)/shard_map/dot_general | solution.py:98
  54.2 7.6 %all-reduce.1 = (f32[768]{0:T(1024)}, f32[768]{0:T(1024)}) all-reduce(f32[768]{0:T(1024)} %get-tuple-element.5, f32[768]{0:T(1024)} %get-tuple-element.4), channel_id=1, replica_groups=mesh['dp'=8,'neg'=4] {'neg'}, use_global_device_ids=true, to_apply=%region_10.11 | all-reduce | flops 1536 | bytes 12288 | tf_op jit(solution)/shard_map/psum | solution.py:102
  61.8 1.3 convert_divide_fusion
  63.1 0.7 add_select_fusion.2
  63.8 4.3 %select_convert_fusion = bf16[768,2048]{1,0:T(8,128)(2,1)S(1)} fusion(f32[768,2048]{1,0:T(8,128)} %get-tuple-element.39, f32[768]{0:T(1024)S(1)} %get-tuple-element.28, bf16[768]{0:T(1024)(128)(2,1)S(1)} %add_select_fusion.2, f32[2048]{0:T(1024)} %fusion.3, s32[768]{0:T(1024)} %broadcast_subtract_fusion), kind=kLoop, calls=%fused_computation | loop fusion | flops 9437184 | bytes 9453056 | tf_op jit(solution)/shard_map/convert_element_type | solution.py:112
  68.1 1.9 multiply_convert_fusion.4
  70.0 14.0 %all_to_all.25 = bf16[4,192,512]{2,1,0:T(8,128)(2,1)S(1)} all-to-all(bf16[4,192,512]{2,1,0:T(8,128)(2,1)S(1)} %bitcast.80), channel_id=1, replica_groups=mesh['dp'=8,'neg'=4] {'neg'}, dimensions={0} | all-to-all | bytes 1572864 | tf_op jit(solution)/shard_map/all_to_all | solution.py:37
  84.5 8.0 %all_gather.7 = bf16[768,512]{1,0:T(8,128)(2,1)S(1)} all-gather(bf16[192,512]{1,0:T(8,128)(2,1)S(1)} %multiply_convert_fusion.9), channel_id=1, replica_groups=mesh['dp'=8,'neg'=4] {'neg'}, dimensions={0}, use_global_device_ids=true | all-gather | bytes 983040 | tf_op jit(solution)/shard_map/all_gather | solution.py:122
  92.6 1.2 fusion.17
  93.7 7.0 %all-reduce = (f32[768]{0:T(1024)S(1)}, f32[768]{0:T(1024)S(1)}) all-reduce(f32[768]{0:T(1024)S(1)} %get-tuple-element.9, f32[768]{0:T(1024)S(1)} %get-tuple-element.8), channel_id=1, replica_groups=mesh['dp'=8,'neg'=4] {'neg'}, use_global_device_ids=true, to_apply=%region_18.19 | all-reduce | flops 1536 | bytes 12288 | tf_op jit(solution)/shard_map/psum | solution.py:131
  100.9 0.7 copy-done.17
  101.6 3.1 %multiply_convert_fusion.1 = bf16[2,2,384,384]{3,2,1,0:T(8,128)(2,1)S(1)} fusion(f32[2,2,384,384]{3,2,1,0:T(8,128)} %get-tuple-element.37, f32[2,384,384]{2,1,0:T(8,128)} %copy-done.12, bf16[2,384,2,1,64]{1,0,4,3,2:T(2,128)(2,1)S(1)} %copy-done.21, bf16[2,384,2,64]{1,0,3,2:T(2,128)(2,1)S(1)} %reshape.142), kind=kOutput, calls=%fused_computation.10 | convolution fusion | flops 81985536 | bytes 5111808 | tf_op jit(solution)/shard_map/bihd,bjhd->bhij/dot_general | solution.py:140
  105.1 1.3 convolution_bitcast_fusion.1
  106.4 1.1 convolution_bitcast_fusion.2
  107.4 1.1 convolution_convert_fusion.2
  108.5 1.2 stack_reshape.3
  109.9 2.8 %copy.29 = f32[2,384,2,4,64]{4,3,2,1,0:T(4,128)} copy(f32[2,384,2,4,64]{1,4,2,0,3:T(8,128)S(1)} %pad_maximum_fusion) | data formatting | bytes 3145728 | tf_op jit(solution)/shard_map/reshape | solution.py:161
  112.7 3.5 %reshape.148 = f32[768,512]{1,0:T(8,128)S(1)} reshape(f32[2,384,2,4,64]{4,3,2,1,0:T(4,128)} %copy.29) | data formatting | bytes 3145728 | tf_op jit(solution)/shard_map/reshape | solution.py:161
  116.2 5.8 %all-to-all-start.3 = ((bf16[8,64,128]{2,1,0:T(8,128)(2,1)}), bf16[8,64,128]{2,1,0:T(8,128)(2,1)S(1)}, u32[]{:S(2)}, u32[]{:S(2)}) async-start(bf16[8,64,128]{2,1,0:T(8,128)(2,1)} %bitcast.14), calls=%async_computation.3 | async-start | bytes 262144 | tf_op jit(solution)/shard_map/all_to_all | solution.py:37
  122.1 3.3 %convolution_convert_fusion.1 = bf16[512,512]{1,0:T(8,128)(2,1)} fusion(f32[768,512]{1,0:T(8,128)S(1)} %reshape.148, f32[768,512]{1,0:T(8,128)} %get-tuple-element.35, bf16[768,512]{1,0:T(8,128)(2,1)S(1)} %copy-done.6, f32[768]{0:T(1024)S(1)} %copy-done.30, f32[768]{0:T(1024)S(1)} %copy-done.28), kind=kOutput, calls=%fused_computation.25 | convolution fusion | flops 408027136 | bytes 4462592 | tf_op jit(solution)/shard_map/dot_general | solution.py:163
  125.3 4.0 %all-to-all-done.3 = bf16[8,64,128]{2,1,0:T(8,128)(2,1)S(1)} async-done(((bf16[8,64,128]{2,1,0:T(8,128)(2,1)}), bf16[8,64,128]{2,1,0:T(8,128)(2,1)S(1)}, u32[]{:S(2)}, u32[]{:S(2)}) %all-to-all-start.3) | async-done | bytes 131104 | tf_op jit(solution)/shard_map/all_to_all | solution.py:37
  129.4 3.5 %all-to-all-start.2 = ((bf16[8,64,512]{2,1,0:T(8,128)(2,1)}), bf16[8,64,512]{2,1,0:T(8,128)(2,1)S(1)}, u32[]{:S(2)}, u32[]{:S(2)}) async-start(bf16[8,64,512]{2,1,0:T(8,128)(2,1)} %bitcast.81), calls=%async_computation.2 | async-start | bytes 1048576 | tf_op jit(solution)/shard_map/all_to_all | solution.py:37
  132.9 5.2 %multiply_convert_fusion = bf16[2048,512]{1,0:T(8,128)(2,1)} fusion(bf16[768,2048]{1,0:T(8,128)(2,1)} %copy-done.7, bf16[768,512]{1,0:T(8,128)(2,1)} %copy-done.19), kind=kOutput, calls=%fused_computation.9 | convolution fusion | flops 1612709888 | bytes 6029312 | tf_op jit(solution)/shard_map/dot_general | solution.py:116
  138.1 6.7 %all-to-all-done.2 = bf16[8,64,512]{2,1,0:T(8,128)(2,1)S(1)} async-done(((bf16[8,64,512]{2,1,0:T(8,128)(2,1)}), bf16[8,64,512]{2,1,0:T(8,128)(2,1)S(1)}, u32[]{:S(2)}, u32[]{:S(2)}) %all-to-all-start.2) | async-done | bytes 524320 | tf_op jit(solution)/shard_map/all_to_all | solution.py:37
  144.9 3.7 %all-to-all-start.4 = ((bf16[8,256,512]{2,1,0:T(8,128)(2,1)}), bf16[8,256,512]{2,1,0:T(8,128)(2,1)S(1)}, u32[]{:S(2)}, u32[]{:S(2)}) async-start(bf16[8,256,512]{2,1,0:T(8,128)(2,1)} %bitcast.77), calls=%async_computation.4 | async-start | bytes 4194304 | tf_op jit(solution)/shard_map/all_to_all | solution.py:37
  148.6 3.9 %convert_multiply_fusion = f32[2048,512]{1,0:T(8,128)} fusion(bf16[2048,512]{1,0:T(8,128)(2,1)} %param.13, f32[2048]{0:T(1024)S(1)} %add_rsqrt_fusion), kind=kLoop, calls=%fused_computation.4 | loop fusion | flops 2097152 | bytes 6299648 | tf_op jit(solution)/shard_map/mul | solution.py:27
  152.5 0.6 convert_reduce_fusion.5
  153.1 0.7 convert_reduce_fusion.4
  153.8 41.8 %all-to-all-done.4 = bf16[8,256,512]{2,1,0:T(8,128)(2,1)S(1)} async-done(((bf16[8,256,512]{2,1,0:T(8,128)(2,1)}), bf16[8,256,512]{2,1,0:T(8,128)(2,1)S(1)}, u32[]{:S(2)}, u32[]{:S(2)}) %all-to-all-start.4) | async-done | bytes 2097184 | tf_op jit(solution)/shard_map/all_to_all | solution.py:37
  195.9 1.2 multiply_reduce_fusion.1
  197.1 2.0 %subtract_multiply_fusion = f32[256,512]{1,0:T(8,128)} fusion(f32[256,512]{1,0:T(8,128)S(1)} %convert_reduce_fusion, f32[2048,512]{1,0:T(8,128)} %convert_multiply_fusion, s32[]{:T(128)S(6)} %select_n.37, f32[256]{0:T(256)S(1)} %dynamic-slice.3, f32[256]{0:T(256)S(1)} %multiply_reduce_fusion.1), kind=kLoop, calls=%fused_computation.40 | loop fusion | flops 393216 | bytes 1574916 | tf_op jit(solution)/shard_map/mul | solution.py:31
  (89 shorter events, 3.9 us)
Async XLA Ops:
  0.6 2.3 %copy-start = (bf16[512,512]{1,0:T(8,128)(2,1)S(1)}, bf16[512,512]{1,0:T(8,128)(2,1)}, u32[]{:S(2)}) copy-start(bf16[512,512]{1,0:T(8,128)(2,1)} %param.9) | copy-start | bytes 1572868
  2.9 3.1 %copy-start.27 = (f32[768]{0:T(1024)}, f32[768]{0:T(1024)S(1)}, u32[]{:S(2)}) copy-start(f32[768]{0:T(1024)S(1)} %get-tuple-element.32) | copy-start | bytes 9220
  2.9 3.1 %copy-start.29 = (f32[768]{0:T(1024)}, f32[768]{0:T(1024)S(1)}, u32[]{:S(2)}) copy-start(f32[768]{0:T(1024)S(1)} %get-tuple-element.33) | copy-start | bytes 9220
  7.1 2.5 %copy-start.13 = (bf16[2,384,2,1,64]{1,0,4,3,2:T(2,128)(2,1)}, bf16[2,384,2,1,64]{1,0,4,3,2:T(2,128)(2,1)S(1)}, u32[]{:S(2)}) copy-start(bf16[2,384,2,1,64]{1,0,4,3,2:T(2,128)(2,1)S(1)} %get-tuple-element.25) | copy-start | bytes 589828
  7.1 2.5 %copy-start.15 = (bf16[2,384,2,1,64]{1,0,4,3,2:T(2,128)(2,1)}, bf16[2,384,2,1,64]{1,0,4,3,2:T(2,128)(2,1)S(1)}, u32[]{:S(2)}) copy-start(bf16[2,384,2,1,64]{1,0,4,3,2:T(2,128)(2,1)S(1)} %get-tuple-element.23) | copy-start | bytes 589828
  7.1 2.5 %copy-start.20 = (bf16[2,384,2,1,64]{1,0,4,3,2:T(2,128)(2,1)}, bf16[2,384,2,1,64]{1,0,4,3,2:T(2,128)(2,1)S(1)}, u32[]{:S(2)}) copy-start(bf16[2,384,2,1,64]{1,0,4,3,2:T(2,128)(2,1)S(1)} %get-tuple-element.22) | copy-start | bytes 589828
  7.1 12.1 %copy-start.4 = (f32[16,8,2,384]{3,1,2,0:T(8,128)}, f32[16,8,2,384]{3,1,2,0:T(8,128)S(1)}, u32[]{:S(2)}) copy-start(f32[16,8,2,384]{3,1,2,0:T(8,128)S(1)} %copy.35) | copy-start | bytes 1179652
  7.3 2.3 %copy-start.12 = (f32[2,384,384]{2,1,0:T(8,128)}, f32[2,384,384]{2,1,0:T(8,128)S(1)}, u32[]{:S(2)}) copy-start(f32[2,384,384]{2,1,0:T(8,128)S(1)} %and_convert_fusion) | copy-start | bytes 3538948
  9.6 1.0 copy-start.2
  9.6 9.7 %copy-start.22 = (bf16[128,512]{1,0:T(8,128)(2,1)S(1)}, bf16[128,512]{1,0:T(8,128)(2,1)}, u32[]{:S(2)}) copy-start(bf16[128,512]{1,0:T(8,128)(2,1)} %param.10) | copy-start | bytes 393220
  19.3 1.3 copy-start.8
  20.6 7.4 %copy-start.23 = (s32[4096]{0:T(1024)S(1)}, s32[4096]{0:T(1024)}, u32[]{:S(2)}) copy-start(s32[4096]{0:T(1024)} %param.12) | copy-start | bytes 49156
  20.6 7.4 %copy-start.26 = (s32[768]{0:T(1024)S(1)}, s32[768]{0:T(1024)}, u32[]{:S(2)}) copy-start(s32[768]{0:T(1024)} %param.11) | copy-start | bytes 9220
  20.6 9.3 %copy-start.1 = (bf16[2048,512]{1,0:T(8,128)(2,1)S(1)}, bf16[2048,512]{1,0:T(8,128)(2,1)}, u32[]{:S(2)}) copy-start(bf16[2048,512]{1,0:T(8,128)(2,1)} %param.13) | copy-start | bytes 6291460
  20.6 16.0 %all-to-all-start = ((bf16[4,192,512]{2,1,0:T(8,128)(2,1)}), bf16[4,192,512]{2,1,0:T(8,128)(2,1)}, u32[]{:S(2)}, u32[]{:S(2)}) async-start(bf16[4,192,512]{2,1,0:T(8,128)(2,1)} %bitcast.76), calls=%async_computation | async-start | bytes 1572864 | tf_op jit(solution)/shard_map/all_to_all | solution.py:37
  39.0 0.6 copy-start.24
  47.6 6.5 %copy-start.19 = (bf16[768,512]{1,0:T(8,128)(2,1)}, bf16[768,512]{1,0:T(8,128)(2,1)S(1)}, u32[]{:S(2)}) copy-start(bf16[768,512]{1,0:T(8,128)(2,1)S(1)} %all_gather.6) | copy-start | bytes 2359300
  68.1 1.9 copy-start.7
  70.0 14.2 %copy-start.25 = (f32[192]{0:T(256)S(1)}, f32[192]{0:T(256)}, u32[]{:S(2)}) copy-start(f32[192]{0:T(256)} %copy-done.24) | copy-start | bytes 2308
  84.1 8.5 %copy-start.5 = (f32[16,8,2,384]{3,1,2,0:T(8,128)S(1)}, f32[16,8,2,384]{3,1,2,0:T(8,128)}, u32[]{:S(2)}) copy-start(f32[16,8,2,384]{3,1,2,0:T(8,128)} %copy-done.4) | copy-start | bytes 1179652
  92.6 9.0 %copy-start.21 = (bf16[2,384,2,1,64]{1,0,4,3,2:T(2,128)(2,1)S(1)}, bf16[2,384,2,1,64]{1,0,4,3,2:T(2,128)(2,1)}, u32[]{:S(2)}) copy-start(bf16[2,384,2,1,64]{1,0,4,3,2:T(2,128)(2,1)} %copy-done.20) | copy-start | bytes 589828
  100.9 0.7 copy-start.17
  101.6 3.1 %copy-start.16 = (bf16[2,384,2,1,64]{1,0,4,3,2:T(2,128)(2,1)S(1)}, bf16[2,384,2,1,64]{1,0,4,3,2:T(2,128)(2,1)}, u32[]{:S(2)}) copy-start(bf16[2,384,2,1,64]{1,0,4,3,2:T(2,128)(2,1)} %copy-done.15) | copy-start | bytes 589828
  101.6 3.5 %copy-start.14 = (bf16[2,384,2,1,64]{1,0,4,3,2:T(2,128)(2,1)S(1)}, bf16[2,384,2,1,64]{1,0,4,3,2:T(2,128)(2,1)}, u32[]{:S(2)}) copy-start(bf16[2,384,2,1,64]{1,0,4,3,2:T(2,128)(2,1)} %copy-done.13) | copy-start | bytes 589828
  104.7 1.6 copy-start.3
  104.7 1.6 copy-start.18
  105.1 2.4 %copy-start.9 = (bf16[768,128]{0,1:T(8,128)(2,1)S(1)}, bf16[768,128]{0,1:T(8,128)(2,1)}, u32[]{:S(2)}) copy-start(bf16[768,128]{0,1:T(8,128)(2,1)} %copy-done.8) | copy-start | bytes 589828
  107.4 2.3 %copy-start.10 = (f32[2,384,2,1,64]{1,4,2,0,3:T(8,128)S(1)}, f32[2,384,2,1,64]{1,4,2,0,3:T(8,128)}, u32[]{:S(2)}) copy-start(f32[2,384,2,1,64]{1,4,2,0,3:T(8,128)} %convolution_bitcast_fusion.1) | copy-start | bytes 1179652
  107.4 2.3 %copy-start.11 = (f32[2,384,2,1,64]{1,4,2,0,3:T(8,128)S(1)}, f32[2,384,2,1,64]{1,4,2,0,3:T(8,128)}, u32[]{:S(2)}) copy-start(f32[2,384,2,1,64]{1,4,2,0,3:T(8,128)} %convolution_bitcast_fusion.2) | copy-start | bytes 1179652
  112.7 9.4 %copy-start.6 = (bf16[768,512]{1,0:T(8,128)(2,1)S(1)}, bf16[768,512]{1,0:T(8,128)(2,1)}, u32[]{:S(2)}) copy-start(bf16[768,512]{1,0:T(8,128)(2,1)} %param.7) | copy-start | bytes 2359300
  112.7 9.4 %copy-start.28 = (f32[768]{0:T(1024)S(1)}, f32[768]{0:T(1024)}, u32[]{:S(2)}) copy-start(f32[768]{0:T(1024)} %copy-done.27) | copy-start | bytes 9220
  112.7 9.4 %copy-start.30 = (f32[768]{0:T(1024)S(1)}, f32[768]{0:T(1024)}, u32[]{:S(2)}) copy-start(f32[768]{0:T(1024)} %copy-done.29) | copy-start | bytes 9220
  116.2 13.2 %all-to-all-start.3 = ((bf16[8,64,128]{2,1,0:T(8,128)(2,1)}), bf16[8,64,128]{2,1,0:T(8,128)(2,1)S(1)}, u32[]{:S(2)}, u32[]{:S(2)}) async-start(bf16[8,64,128]{2,1,0:T(8,128)(2,1)} %bitcast.14), calls=%async_computation.3 | async-start | bytes 262144 | tf_op jit(solution)/shard_map/all_to_all | solution.py:37
  129.4 15.5 %all-to-all-start.2 = ((bf16[8,64,512]{2,1,0:T(8,128)(2,1)}), bf16[8,64,512]{2,1,0:T(8,128)(2,1)S(1)}, u32[]{:S(2)}, u32[]{:S(2)}) async-start(bf16[8,64,512]{2,1,0:T(8,128)(2,1)} %bitcast.81), calls=%async_computation.2 | async-start | bytes 1048576 | tf_op jit(solution)/shard_map/all_to_all | solution.py:37
  144.9 50.7 %all-to-all-start.4 = ((bf16[8,256,512]{2,1,0:T(8,128)(2,1)}), bf16[8,256,512]{2,1,0:T(8,128)(2,1)S(1)}, u32[]{:S(2)}, u32[]{:S(2)}) async-start(bf16[8,256,512]{2,1,0:T(8,128)(2,1)} %bitcast.77), calls=%async_computation.4 | async-start | bytes 4194304 | tf_op jit(solution)/shard_map/all_to_all | solution.py:37
where the time goes:
time: 200 us; the launch traced here: 199 us
  waiting for transfers between devices  58.7 us (29%)
  blocking collectives  53.1 us (27%)
  matrix products  33.5 us (17%)
  other arithmetic  24.8 us (12%)
  starting transfers between devices  17.3 us (9%)
  local copies, waits for them, and re-layouts  10.5 us (5%)
    all_to_all x4, waiting for transfers between devices, scatter_sum(): received = lax.all_to_all(parts, axis_name, 0, 0)  58.7 us
    all_to_all x4, starting transfers between devices, scatter_sum(): received = lax.all_to_all(parts, axis_name, 0, 0)  17.3 us
    all_to_all x1, blocking collectives, scatter_sum(): received = lax.all_to_all(parts, axis_name, 0, 0)  14 us
    psum x1, blocking collectives, on_device(): lax.psum((jnp.sum(attended, -1), jnp.sum(attended * attended, -1)), 'neg')  8.55 us
    all_gather x1, blocking collectives, on_device(): output_rounded = lax.all_gather(output_part, 'neg', axis=0, tiled=True)  8.01 us
    all_gather x1, blocking collectives, on_device(): lax.all_gather(user_unit.astype(jnp.bfloat16), 'neg', axis=0, tiled=True)  7.9 us
    psum x1, blocking collectives, on_device(): lax.psum((jnp.sum(jnp.where(is_target, logits, 0.0), -1), jnp.sum(exp_ter...  7.63 us
    psum x1, blocking collectives, on_device(): lax.psum((jnp.sum(centred_grad, -1), jnp.sum(centred_grad * centred, -1))...  6.99 us
  transfers between devices with their start and end apart: 4, of which 4 were waited for; matrix products, arithmetic and copies ran while one was open for 10% of the time, Pallas kernels for 0%

commit v1 on v0

--- a/solution.py
+++ b/solution.py
@@ -1,6 +1,11 @@
+import functools
+from types import SimpleNamespace
+
 import jax
 import jax.numpy as jnp
 from jax import lax
+from jax.experimental import pallas as pl
+from jax.experimental.pallas import tpu as pltpu
 from jax.sharding import PartitionSpec as P
 
 HEAD = 64
@@ -48,7 +53,7 @@
     return table.reshape(1, row_count)
 
 
-def on_device(history, lengths, w_in, w_out, target_ids, negative_ids, item_table):
+def plain_device(history, lengths, w_in, w_out, target_ids, negative_ids, item_table):
     tok_rows, model_width = history.shape
     user_count = lengths.shape[0]
     hist_len = tok_rows // user_count
@@ -178,6 +183,628 @@
     return (token_loss, grad_w_in, grad_w_out, grad_table)
 
 
+MESH = pl.DeviceIdType.MESH
+LANES = 128
+f32 = jnp.float32
+bf16 = jnp.bfloat16
+
+
+def dot_nn(a, b):
+    return lax.dot_general(a, b, (((1,), (0,)), ((), ())), preferred_element_type=f32)
+
+
+def dot_nt(a, b):
+    return lax.dot_general(a, b, (((1,), (1,)), ((), ())), preferred_element_type=f32)
+
+
+def dot_tn(a, b):
+    return lax.dot_general(a, b, (((0,), (0,)), ((), ())), preferred_element_type=f32)
+
+
+def rows_to_columns(rows):
+    length = rows[0].shape[1]
+    place = lax.broadcasted_iota(jnp.int32, (LANES, length), 0)
+    packed = jnp.zeros((LANES, length), f32)
+    for index, row in enumerate(rows):
+        packed = jnp.where(place == index, row, packed)
+    return packed.T
+
+
+def columns_to_rows(columns):
+    length = columns[0].shape[0]
+    place = lax.broadcasted_iota(jnp.int32, (length, LANES), 1)
+    packed = jnp.zeros((length, LANES), f32)
+    for index, column in enumerate(columns):
+        packed = jnp.where(place == index, column, packed)
+    return packed.T[:8]
+
+
+def plan(history, lengths, w_in, w_out, item_table, negative_ids, dp_size, neg_size):
+    s = SimpleNamespace()
+    s.P, s.N = dp_size, neg_size
+    s.Y = neg_size // 2
+    grid_x = 1
+    while grid_x * grid_x * 4 <= dp_size:
+        grid_x *= 2
+    s.X, s.Z = grid_x, dp_size // grid_x
+    s.U = lengths.shape[0]
+    s.H = history.shape[0] // lengths.shape[0]
+    s.D = history.shape[1]
+    s.lw = w_out.shape[0]
+    s.I = item_table.shape[0]
+    s.NB = negative_ids.shape[0]
+    s.share = s.H // neg_size
+    s.tshare = s.I // dp_size
+    s.wshare = s.D // dp_size
+    s.CH = 4 * LANES
+    return s
+
+
+def fits(s):
+    return (
+        s.lw % LANES == 0
+        and s.tshare % LANES == 0
+        and s.H % LANES == 0
+        and s.I % s.CH == 0
+        and s.D % LANES == 0
+        and s.share % 16 == 0
+        and s.share <= LANES
+        and s.wshare % 16 == 0
+        and s.N % 2 == 0
+        and s.X * s.Z == s.P
+    )
+
+
+def scratch_of(s):
+    U, H, D, lw, I, N, Y, X, Z = s.U, s.H, s.D, s.lw, s.I, s.N, s.Y, s.X, s.Z
+    lh, share, tshare, wshare, CH = lw // HEAD, s.share, s.tshare, s.wshare, s.CH
+    X1, Z1, Y1 = max(X - 1, 1), max(Z - 1, 1), max(Y - 1, 1)
+    V = pltpu.VMEM
+    return dict(
+        item_v=V((I, D), bf16),
+        item_r=V((I, D), bf16),
+        wperm=V((D, 4 * lw), bf16),
+        normed=V((U, H, D), bf16),
+        normed_t=V((D, U * H), bf16),
+        pre=V((U, H, 4 * lw), f32),
+        proj=V((U, H, 4 * lw), bf16),
+        scores=V((U, lh, H, H), f32),
+        attn=V((U, lh, H, H), bf16),
+        att=V((U, H, lw), f32),
+        norm_col=V((U, H, LANES), f32),
+        stat=V((U, N, 8, H), f32),
+        wout_all=V((N, lw, D), bf16),
+        mixed_all=V((U, N, H, lw), bf16),
+        gate_rows=V((U, N, share, lw), bf16),
+        out=V((U, H, D), f32),
+        u64=V((U, H, D), bf16),
+        exps=V((U * H, I), bf16),
+        hot=V((U * H, I), bf16),
+        tid_col=V((U, H, LANES), f32),
+        counts=V((I // CH, 1, CH), f32),
+        tgt=V((U, H, D), f32),
+        acc=V((U, H, D), f32),
+        nacc=V((H, LANES), f32),
+        zst=V((U, N, 8, H), f32),
+        up=V((U, Y, share, D), bf16),
+        r1=V((U, Y, share, D), bf16),
+        s2=V((U, Y1, share, D), bf16),
+        r2=V((U, Y1, share, D), bf16),
+        og_all=V((U, N, share, D), bf16),
+        mg_send=V((U, N, share, lw), bf16),
+        mg_recv=V((U, N, share, lw), bf16),
+        bs_send=V((U, 8, LANES), f32),
+        bs_recv=V((U, N, 8, LANES), f32),
+        ru_t=V((D, U * H), bf16),
+        row_send=V((Z, X1, D, tshare), bf16),
+        row_own=V((Z, D, tshare), f32),
+        row_rx=V((Z, X1, D, tshare), bf16),
+        row_zs=V((Z1, D, tshare), bf16),
+        row_rz=V((Z1, D, tshare), bf16),
+        g_acc=V((D, 5 * lw), f32),
+        g_send=V((Z, X1, wshare, 5 * lw), bf16),
+        g_rx=V((Z, X1, wshare, 5 * lw), bf16),
+        g_zs=V((Z1, wshare, 5 * lw), bf16),
+        g_rz=V((Z1, wshare, 5 * lw), bf16),
+        item_sem=pltpu.SemaphoreType.DMA(()),
+        ssem=pltpu.SemaphoreType.DMA((192,)),
+        rsem=pltpu.SemaphoreType.DMA((192,)),
+    )
+
+
+def mega(s, names, hist_ref, len_ref, w_in_ref, w_out_ref, tid_ref, nid_ref, item_hbm,
+         loss_ref, gwin_ref, gwout_ref, gtab_ref, *scratch):
+    R = SimpleNamespace(**dict(zip(names, scratch)))
+    U, H, D, lw, I, N, Y, X, Z = s.U, s.H, s.D, s.lw, s.I, s.N, s.Y, s.X, s.Z
+    lh, share, tshare, wshare, CH = lw // HEAD, s.share, s.tshare, s.wshare, s.CH
+    me_dp = lax.axis_index("dp")
+    n = lax.axis_index("neg")
+    y, core = lax.div(n, 2), lax.rem(n, 2)
+    partner = y * 2 + (1 - core)
+    z, x = lax.div(me_dp, X), lax.rem(me_dp, X)
+
+    def at_neg(index):
+        return (me_dp, index)
+
+    def turn(index, step, size):
+        return lax.rem(index + step, size)
+
+    neg_peers = [turn(n, k, N) for k in range(1, N)]
+    x_peers = [(z * X + turn(x, k, X), n) for k in range(1, X)]
+    z_peers = [(turn(z, k, Z) * X + x, n) for k in range(1, Z)]
+    everyone = [at_neg(p) for p in neg_peers] + x_peers + z_peers
+
+    barrier = pltpu.get_barrier_semaphore()
+    for peer in everyone:
+        pl.semaphore_signal(barrier, inc=1, device_id=peer, device_id_type=MESH)
+
+    sent = []
+
+    def send(src, dst, peer):
+        index = len(sent)
+        copy = pltpu.make_async_remote_copy(
+            src_ref=src,
+            dst_ref=dst,
+            send_sem=R.ssem.at[index],
+            recv_sem=R.rsem.at[index],
+            device_id=peer,
+            device_id_type=MESH,
+        )
+        copy.start()
+        sent.append(copy)
+        return copy
+
+    item_copy = pltpu.make_async_copy(item_hbm, R.item_v, R.item_sem)
+    item_copy.start()
+
+    w_in = w_in_ref[...]
+    pieces = []
+    for part in range(4):
+        for h in range(lh):
+            first = (h * 4 + part) * HEAD
+            pieces.append(w_in[:, first : first + HEAD])
+    R.wperm[...] = jnp.concatenate(pieces, axis=1)
+
+    head_lane = lax.div(lax.broadcasted_iota(jnp.int32, (1, lw), 1), HEAD)
+    head_mask = [jnp.where(head_lane == h, 1.0, 0.0).astype(bf16) for h in range(lh)]
+
+    def attn_mask(b):
+        row = lax.broadcasted_iota(jnp.int32, (H, H), 0)
+        col = lax.broadcasted_iota(jnp.int32, (H, H), 1)
+        return jnp.where((col <= row) & (row < len_ref[b]), 1.0 / H, 0.0)
+
+    def part_of(b, part):
+        return R.proj[b, :, part * lw : (part + 1) * lw]
+
+    def project(b):
+        rows = hist_ref[b * H : (b + 1) * H, :].astype(f32)
+        normed = moment_norm(rows)[0].astype(bf16)
+        R.normed[b] = normed
+        pre = dot_nn(normed, R.wperm[...])
+        R.pre[b] = pre
+        R.proj[b] = (pre * jax.nn.sigmoid(pre)).astype(bf16)
+
+    def attend(b):
+        value, query, key = part_of(b, 1), part_of(b, 2), part_of(b, 3)
+        mask = attn_mask(b)
+        total = jnp.zeros((H, lw), f32)
+        for h in range(lh):
+            scores = dot_nt(query * head_mask[h], key)
+            R.scores[b, h] = scores
+            weights = (scores * jax.nn.sigmoid(scores) * mask).astype(bf16)
+            R.attn[b, h] = weights
+            total = total + dot_nn(weights, value * head_mask[h])
+        R.att[b] = total
+        R.stat[b, n] = columns_to_rows(
+            [jnp.sum(total, -1, keepdims=True), jnp.sum(total * total, -1, keepdims=True)]
+        )
+
+    def send_stats(b):
+        return [send(R.stat.at[b, n], R.stat.at[b, n], at_neg(p)) for p in neg_peers]
+
+    def send_gates(b):
+        return [
+            send(
+                R.proj.at[b, pl.ds(pl.multiple_of(p * share, 16), share), pl.ds(0, lw)],
+                R.gate_rows.at[b, n],
+                at_neg(p),
+            )
+            for p in neg_peers
+        ]
+
+    def gather_start(ref):
+        to_partner = send(ref.at[n], ref.at[n], at_neg(partner))
+        along_y = [send(ref.at[n], ref.at[n], at_neg(turn(y, k, Y) * 2 + core)) for k in range(1, Y)]
+        return to_partner, along_y
+
+    def gather_relay(ref, state):
+        relays = []
+        for k in range(1, Y):
+            state[1][k - 1].wait_recv()
+            source = turn(y, Y - k, Y) * 2 + core
+            relays.append(send(ref.at[source], ref.at[source], at_neg(partner)))
+        return relays
+
+    def gather_wait(state, relays):
+        state[0].wait_recv()
+        for copy in relays:
+            copy.wait_recv()
+
+    project(0)
+    pl.semaphore_wait(barrier, len(everyone))
+    R.wout_all[n] = w_out_ref[...]
+    wout_state = gather_start(R.wout_all)
+    attend(0)
+    stat_copies = [send_stats(0)]
+    project(1)
+    attend(1)
+    for b in range(1, U):
+        if b > 1:
+            project(b)
+            attend(b)
+        stat_copies.append(send_stats(b))
+
+    item_copy.wait()
+    step_rows = CH
+
+    def norm_items(i, carry):
+        rows = pl.ds(pl.multiple_of(i * step_rows, step_rows), step_rows)
+        R.item_r[rows, :] = normalize_rows(R.item_v[rows, :].astype(f32))[0].astype(bf16)
+        return carry
+
+    lax.fori_loop(0, I // step_rows, norm_items, 0)
+
+    gather_states = []
+    for b in range(U):
+        for copy in stat_copies[b]:
+            copy.wait_recv()
+        total = R.stat[b, 0]
+        for d in range(1, N):
+            total = total + R.stat[b, d]
+        mean = total[0:1] / D
+        scale = lax.rsqrt(total[1:2] / D - mean * mean + epsilon)
+        columns = rows_to_columns([mean, scale])
+        R.norm_col[b] = columns
+        centred = (R.att[b] - columns[:, 0:1]) * columns[:, 1:2]
+        R.att[b] = centred
+        R.mixed_all[b, n] = (centred * part_of(b, 0).astype(f32)).astype(bf16)
+        gather_states.append(gather_start(R.mixed_all.at[b]))
+    gate_copies = [send_gates(b) for b in range(U)]
+    for b in range(U):
+        R.gate_rows[b, n] = R.proj[b, pl.ds(pl.multiple_of(n * share, 16), share), 0:lw]
+
+    slots = nid_ref[...] - n * I
+    high = lax.shift_right_logical(slots, 7)
+    low = lax.bitwise_and(slots, LANES - 1)
+    coarse = jnp.where(
+        high == lax.broadcasted_iota(jnp.int32, (I // LANES, slots.shape[1]), 0), 1.0, 0.0
+    ).astype(bf16)
+    fine = jnp.where(
+        low == lax.broadcasted_iota(jnp.int32, (LANES, slots.shape[1]), 0), 1.0, 0.0
+    ).astype(bf16)
+    table = dot_nt(coarse, fine)
+    groups = CH // LANES
+    for i in range(I // CH):
+        R.counts[i] = jnp.concatenate(
+            [table[i * groups + g : i * groups + g + 1, :] for g in range(groups)], axis=1
+        )
+
+    def is_target(b, i):
+        ids = jnp.concatenate([R.tid_col[b]] * groups, axis=1)
+        place = lax.broadcasted_iota(jnp.int32, (H, CH), 1) + i * CH
+        return ids == place.astype(f32)
+
+    def targets(b):
+        ids = (tid_ref[b : b + 1, :] - n * I).astype(f32)
+        R.tid_col[b] = jnp.broadcast_to(ids, (LANES, H)).T
+        R.tgt[b] = jnp.zeros((H, D), f32)
+
+        def body(i, carry):
+            cols = pl.ds(pl.multiple_of(i * CH, CH), CH)
+            hot = jnp.where(is_target(b, i), 1.0, 0.0).astype(bf16)
+            R.hot[b * H : (b + 1) * H, cols] = hot
+            R.tgt[b] += dot_nn(hot, R.item_r[cols, :])
+            return carry
+
+        lax.fori_loop(0, I // CH, body, 0)
+
+    wout_relays = gather_relay(R.wout_all, wout_state)
+    targets(0)
+    relays = [gather_relay(R.mixed_all.at[0], gather_states[0])]
+    for b in range(1, U):
+        targets(b)
+        relays.append(gather_relay(R.mixed_all.at[b], gather_states[b]))
+
+    for b in range(U):
+        R.normed_t[:, b * H : (b + 1) * H] = R.normed[b].astype(f32).T.astype(bf16)
+        mask = attn_mask(b)
+        for h in range(lh):
+            R.scores[b, h] = silu_grad(R.scores[b, h]) * mask
+
+    gather_wait(wout_state, wout_relays)
+    z_copies = []
+    for b in range(U):
+        gather_wait(gather_states[b], relays[b])
+        mixed = jnp.concatenate([R.mixed_all[b, d] for d in range(N)], axis=1)
+        w_out_full = R.wout_all[...].reshape(N * lw, D)
+        output = hist_ref[b * H : (b + 1) * H, :].astype(f32) + dot_nn(mixed, w_out_full)
+        R.out[b] = output
+        unit = normalize_rows(output)[0].astype(bf16)
+        scaled = unit * jnp.asarray(logit_scale, bf16)
+        R.u64[b] = scaled
+        positive = jnp.sum(scaled.astype(f32) * R.tgt[b], -1, keepdims=True)
+        R.acc[b] = jnp.zeros((H, D), f32)
+        R.nacc[...] = jnp.zeros((H, LANES), f32)
+
+        def body(i, carry, b=b):
+            cols = pl.ds(pl.multiple_of(i * CH, CH), CH)
+            items = R.item_r[cols, :]
+            terms = jnp.exp(dot_nt(R.u64[b], items)) * R.counts[i]
+            terms = jnp.where(is_target(b, i), 0.0, terms)
+            partial = terms[:, 0:LANES]
+            for g in range(1, groups):
+                partial = partial + terms[:, g * LANES : (g + 1) * LANES]
+            R.nacc[...] += partial
+            half = terms.astype(bf16)
+            R.exps[b * H : (b + 1) * H, cols] = half
+            R.acc[b] += dot_nn(half, items)
+            return carry
+
+        lax.fori_loop(0, I // CH, body, 0)
+        negative = jnp.sum(R.nacc[...], -1, keepdims=True)
+        R.zst[b, n] = columns_to_rows([negative, positive])
+        z_copies.append([send(R.zst.at[b, n], R.zst.at[b, n], at_neg(p)) for p in neg_peers])
+
+    r1_copies = []
+    for b in range(U):
+        for copy in z_copies[b]:
+            copy.wait_recv()
+        total = R.zst[b, 0]
+        for d in range(1, N):
+            total = total + R.zst[b, d]
+        negative, positive = total[0:1], total[1:2]
+        partition = jnp.exp(positive) + negative
+        live = lax.broadcasted_iota(jnp.int32, (1, H), 1) < len_ref[b]
+        loss_ref[b : b + 1, :] = jnp.where(live, jnp.log(partition) - positive, 0.0)
+        factor = jnp.where(live, 1.0 / partition, 0.0)
+        columns = rows_to_columns([factor, -negative])
+        factor_col, negative_col = columns[:, 0:1], columns[:, 1:2]
+        unit_part = (logit_scale * factor_col) * (R.acc[b] + negative_col * R.tgt[b])
+        R.acc[b] = unit_part
+        copies = []
+        for other in range(Y):
+            first = pl.multiple_of((other * 2 + (1 - core)) * share, 8)
+            R.up[b, other] = R.acc[b, pl.ds(first, share), :].astype(bf16)
+            copies.append(send(R.up.at[b, other], R.r1.at[b, other], at_neg(partner)))
+        r1_copies.append(copies)
+        scaled_rows = R.u64[b].astype(f32) * factor_col
+        R.ru_t[:, b * H : (b + 1) * H] = scaled_rows.T.astype(bf16)
+        negative_half = negative_col.astype(bf16)
+
+        def fix(i, carry, b=b, negative_half=negative_half):
+            cols = pl.ds(pl.multiple_of(i * CH, CH), CH)
+            R.exps[b * H : (b + 1) * H, cols] += (
+                R.hot[b * H : (b + 1) * H, cols] * negative_half
+            )
+            return carry
+
+        lax.fori_loop(0, I // CH, fix, 0)
+
+    r2_copies = []
+
+    def share_rows(owner):
+        return pl.ds(pl.multiple_of(owner * share, 8), share)
+
+    for b in range(U):
+        for copy in r1_copies[b]:
+            copy.wait_recv()
+        copies = []
+        for k in range(1, Y):
+            other = turn(y, k, Y)
+            R.s2[b, k - 1] = (
+                R.acc[b, share_rows(other * 2 + core), :] + R.r1[b, other].astype(f32)
+            ).astype(bf16)
+            copies.append(send(R.s2.at[b, k - 1], R.r2.at[b, k - 1], at_neg(other * 2 + core)))
+        r2_copies.append(copies)
+
+    def row_block(index):
+        cols = pl.ds(pl.multiple_of(index * tshare, LANES), tshare)
+        return dot_nn(R.ru_t[...], R.exps[:, cols])
+
+    z_order = list(range(1, Z)) + [0]
+    row_x = dict()
+    for kz in z_order:
+        for kx in range(1, X):
+            target = turn(z, kz, Z) * X + turn(x, kx, X)
+            R.row_send[kz, kx - 1] = row_block(target).astype(bf16)
+            row_x[kz, kx] = send(
+                R.row_send.at[kz, kx - 1], R.row_rx.at[kz, kx - 1], x_peers[kx - 1]
+            )
+
+    mg_copies, og_copies = [], []
+    for b in range(U):
+        for copy in r2_copies[b]:
+            copy.wait_recv()
+        grad = R.acc[b, share_rows(n), :] + R.r1[b, y].astype(f32)
+        for k in range(1, Y):
+            grad = grad + R.r2[b, k - 1].astype(f32)
+        unit, inverse = normalize_rows(R.out[b, share_rows(n), :])
+        half = project_rows(grad, unit, inverse).astype(bf16)
+        R.og_all[b, n] = half
+        sum_g = jnp.zeros((share, 1), f32)
+        sum_gc = jnp.zeros((share, 1), f32)
+        for d in range(N):
+            mixed_grad = dot_nt(half, R.wout_all[d])
+            R.mg_send[b, d] = mixed_grad.astype(bf16)
+            if b == 0 and d == 0:
+                for copies in gate_copies:
+                    for copy in copies:
+                        copy.wait_recv()
+            sum_g = sum_g + jnp.sum(mixed_grad * R.gate_rows[b, d].astype(f32), -1, keepdims=True)
+            mixed = R.mixed_all[b, d, share_rows(n), :].astype(f32)
+            sum_gc = sum_gc + jnp.sum(mixed_grad * mixed, -1, keepdims=True)
+        lane = lax.broadcasted_iota(jnp.int32, (share, LANES), 1)
+        packed = jnp.where(lane == 0, sum_g, jnp.where(lane == 1, sum_gc, 0.0)) / D
+        if share < LANES:
+            packed = jnp.concatenate([packed, jnp.zeros((LANES - share, LANES), f32)], axis=0)
+        sums = packed.T[:8]
+        R.bs_send[b] = sums
+        R.bs_recv[b, n] = sums
+        R.mg_recv[b, n] = R.mg_send[b, n]
+        copies = []
+        for p in neg_peers:
+            copies.append(send(R.mg_send.at[b, p], R.mg_recv.at[b, n], at_neg(p)))
+            copies.append(send(R.bs_send.at[b], R.bs_recv.at[b, n], at_neg(p)))
+        mg_copies.append(copies)
+    for b in range(U):
+        og_copies.append([send(R.og_all.at[b, n], R.og_all.at[b, n], at_neg(p)) for p in neg_peers])
+
+    for kz in z_order:
+        R.row_own[kz] = row_block(turn(z, kz, Z) * X + x)
+
+    row_z = []
+
+    def row_forward(kz):
+        block = R.row_own[kz]
+        for kx in range(1, X):
+            row_x[kz, kx].wait_recv()
+            block = block + R.row_rx[kz, kx - 1].astype(f32)
+        if kz == 0:
+            R.row_own[0] = block
+        else:
+            R.row_zs[kz - 1] = block.astype(bf16)
+            row_z.append(send(R.row_zs.at[kz - 1], R.row_rz.at[kz - 1], z_peers[kz - 1]))
+
+    def backward(b):
+        for copy in mg_copies[b]:
+            copy.wait_recv()
+        mixed_grad = R.mg_recv[b].reshape(H, lw).astype(f32)
+        sums = []
+        for d in range(N):
+            rows = R.bs_recv[b, d]
+            square = jnp.concatenate([rows, jnp.zeros((LANES - 8, LANES), f32)], axis=0).T
+            sums.append(square[:share, :])
+        sums = jnp.concatenate(sums, axis=0)
+        gate = part_of(b, 0).astype(f32)
+        value, query, key = part_of(b, 1), part_of(b, 2), part_of(b, 3)
+        centred = R.att[b]
+        scale = R.norm_col[b][:, 1:2]
+        grad = mixed_grad * gate
+        attended_grad = (scale * (grad - sums[:, 0:1] - centred * sums[:, 1:2])).astype(bf16)
+        value_grad = jnp.zeros((H, lw), f32)
+        query_grad = jnp.zeros((H, lw), f32)
+        key_grad = jnp.zeros((H, lw), f32)
+        for h in range(lh):
+            own = attended_grad * head_mask[h]
+            value_grad = value_grad + dot_tn(R.attn[b, h], own)
+            score_grad = (dot_nt(own, value) * R.scores[b, h]).astype(bf16)
+            query_grad = query_grad + dot_nn(score_grad, key * head_mask[h])
+            key_grad = key_grad + dot_tn(score_grad, query * head_mask[h])
+        project_grad = jnp.concatenate([mixed_grad * centred, value_grad, query_grad, key_grad], axis=1)
+        pre_grad = (project_grad * silu_grad(R.pre[b])).astype(bf16)
+        part = dot_nn(R.normed_t[:, b * H : (b + 1) * H], pre_grad)
+        if b == 0:
+            R.g_acc[:, 0 : 4 * lw] = part
+        else:
+            R.g_acc[:, 0 : 4 * lw] += part
+
+    row_forward(z_order[0])
+    backward(0)
+    if Z > 1:
+        row_forward(z_order[1])
+    for b in range(1, U):
+        backward(b)
+    grad_out = jnp.zeros((lw, D), f32)
+    for b in range(U):
+        for copy in og_copies[b]:
+            copy.wait_recv()
+        grad_out = grad_out + dot_tn(R.mixed_all[b, n], R.og_all[b].reshape(H, D))
+    R.g_acc[:, 4 * lw : 5 * lw] = grad_out.T
+
+    def g_rows(index):
+        return R.g_acc[pl.ds(pl.multiple_of(index * wshare, 8), wshare), :]
+
+    g_x, g_z = dict(), []
+    for kz in z_order:
+        for kx in range(1, X):
+            target = turn(z, kz, Z) * X + turn(x, kx, X)
+            R.g_send[kz, kx - 1] = g_rows(target).astype(bf16)
+            g_x[kz, kx] = send(R.g_send.at[kz, kx - 1], R.g_rx.at[kz, kx - 1], x_peers[kx - 1])
+    for kz in z_order[2:]:
+        row_forward(kz)
+    own_g = None
+    for kz in z_order:
+        block = g_rows(turn(z, kz, Z) * X + x)
+        for kx in range(1, X):
+            g_x[kz, kx].wait_recv()
+            block = block + R.g_rx[kz, kx - 1].astype(f32)
+        if kz == 0:
+            own_g = block
+        else:
+            R.g_zs[kz - 1] = block.astype(bf16)
+            g_z.append(send(R.g_zs.at[kz - 1], R.g_rz.at[kz - 1], z_peers[kz - 1]))
+
+    for copy in row_z:
+        copy.wait_recv()
+    row_total = R.row_own[0]
+    for k in range(Z - 1):
+        row_total = row_total + R.row_rz[k].astype(f32)
+    own_items = R.item_v[pl.ds(pl.multiple_of(me_dp * tshare, 16), tshare), :].astype(f32)
+    unit, inverse = normalize_rows(own_items)
+    gtab_ref[...] = project_rows(row_total.T, unit, inverse)
+
+    for copy in g_z:
+        copy.wait_recv()
+    for k in range(Z - 1):
+        own_g = own_g + R.g_rz[k].astype(f32)
+    pieces = []
+    for h in range(lh):
+        for part in range(4):
+            first = part * lw + h * HEAD
+            pieces.append(own_g[:, first : first + HEAD])
+    gwin_ref[...] = jnp.concatenate(pieces, axis=1)
+    gwout_ref[...] = own_g[:, 4 * lw : 5 * lw]
+    for copy in sent:
+        copy.wait_send()
+
+
+def on_device(dp_size, neg_size, history, lengths, w_in, w_out, target_ids, negative_ids, item_table):
+    s = plan(history, lengths, w_in, w_out, item_table, negative_ids, dp_size, neg_size)
+    if not fits(s):
+        return plain_device(
+            history, lengths, w_in, w_out, target_ids, negative_ids, item_table
+        )
+    scratch = scratch_of(s)
+    vmem = pl.BlockSpec(memory_space=pltpu.VMEM)
+    smem = pl.BlockSpec(memory_space=pltpu.SMEM)
+    U, H, D, lw = s.U, s.H, s.D, s.lw
+    loss, grad_in, grad_out, grad_table = pl.pallas_call(
+        functools.partial(mega, s, tuple(scratch)),
+        out_shape=(
+            jax.ShapeDtypeStruct((U, H), f32),
+            jax.ShapeDtypeStruct((s.wshare, 4 * lw), f32),
+            jax.ShapeDtypeStruct((s.wshare, lw), f32),
+            jax.ShapeDtypeStruct((s.tshare, D), f32),
+        ),
+        in_specs=[vmem, smem, vmem, vmem, vmem, vmem, pl.BlockSpec(memory_space=pl.ANY)],
+        out_specs=(vmem, vmem, vmem, vmem),
+        scratch_shapes=list(scratch.values()),
+        compiler_params=pltpu.CompilerParams(
+            collective_id=0, has_side_effects=True, vmem_limit_bytes=60 * 1024 * 1024
+        ),
+        name="mega",
+    )(
+        history,
+        lengths,
+        w_in,
+        w_out,
+        target_ids.reshape(U, H),
+        negative_ids.reshape(1, s.NB),
+        item_table,
+    )
+    return (loss.reshape(U * H), grad_in, grad_out.T, grad_table)
+
+
 def solution(mesh):
     placed = (
         P("dp", None),
@@ -189,7 +816,7 @@
         P("neg", None),
     )
     return jax.shard_map(
-        on_device,
+        functools.partial(on_device, mesh.shape["dp"], mesh.shape["neg"]),
         mesh=mesh,
         in_specs=placed,
         out_specs=(P("dp"), P("dp", "neg"), P("neg", "dp"), P(("neg", "dp"), None)),

time: 200 us -> 82.9 us (0.41)
  Pallas kernels: 0 us -> 74.6 us
  waiting for transfers between devices: 58.7 us -> 0 us
  blocking collectives: 53.1 us -> 0 us
  matrix products: 33.5 us -> 0 us
  other arithmetic: 24.8 us -> 0 us
  starting transfers between devices: 17.3 us -> 0 us
  local copies, waits for them, and re-layouts: 10.5 us -> 7.35 us
    pallas_call x0 -> x1, Pallas kernels: none -> 74.6 us  [on_device(): pl.pallas_call(functools.partial(mega, s, tuple(scratch)), out_shape=(jax...]
    all_to_all x4 -> x0, waiting for transfers between devices: 58.7 us -> none  [scatter_sum(): received = lax.all_to_all(parts, axis_name, 0, 0)]
    dot_general x15 -> x0, matrix products: 33.5 us -> none  [the longest x1 6.53 us: on_device(): lax.dot_general(user_rounded, item_rounded, (((1,), (1,)), ((), ())), pre...]
    psum x3 -> x0, blocking collectives: 23.2 us -> none  [the longest x1 8.55 us: on_device(): lax.psum((jnp.sum(attended, -1), jnp.sum(attended * attended, -1)), 'neg')]
    all_to_all x4 -> x0, starting transfers between devices: 17.3 us -> none  [scatter_sum(): received = lax.all_to_all(parts, axis_name, 0, 0)]
    all_gather x2 -> x0, blocking collectives: 15.9 us -> none  [the longest x1 8.01 us: on_device(): output_rounded = lax.all_gather(output_part, 'neg', axis=0, tiled=True)]
    all_to_all x1 -> x0, blocking collectives: 14 us -> none  [scatter_sum(): received = lax.all_to_all(parts, axis_name, 0, 0)]
    reduce_sum x10 -> x0, other arithmetic: 7.44 us -> none  [the longest x5 3.04 us: scatter_sum(): return jnp.sum(received.astype(jnp.float32), 0)]
  transfers between devices with their start and end apart: 4 -> 0, of which waited for: 4 -> 0; matrix products, arithmetic and copies ran while one was open for 10% -> 0% of each run, Pallas kernels for 0% -> 0%
where the time goes in v1:
time: 82.9 us; the launch traced here: 82.5 us
  Pallas kernels  74.6 us (90%)
  local copies, waits for them, and re-layouts  7.35 us (9%)
    pallas_call x1, Pallas kernels, on_device(): pl.pallas_call(functools.partial(mega, s, tuple(scratch)), out_shape=(jax...  74.6 us
    unnamed x3, local copies, waits for them, and re-layouts  4.81 us

profile of v1, /device:TPU:0, one launch (start us, length us, event | category | flops | bytes accessed | tf_op | source)
XLA Modules:
  0.0 82.5 jit_solution(12348010579373422379)
XLA Ops:
  0.6 1.3 %reshape.17.tid_ref = s32[2,384]{1,0:T(2,128)} reshape(s32[768]{0:T(1024)} %param.11) | data formatting | bytes 6144 | tf_op jit(solution)/shard_map/reshape | solution.py:801
  1.9 74.6 %mega.1 = (f32[2,384]{1,0:T(2,128)}, f32[64,512]{1,0:T(8,128)}, f32[64,128]{1,0:T(8,128)}, f32[256,512]{1,0:T(8,128)}) custom-call(bf16[768,512]{1,0:T(8,128)(2,1)} %hist_ref.1, s32[2]{0:T(128)} %len_ref.1, bf16[512,512]{1,0:T(8,128)(2,1)} %w_in_ref.1, bf16[128,512]{1,0:T(8,128)(2,1)} %w_out_ref.1, s32[2,384]{1,0:T(2,128)} %reshape.17.tid_ref, ...), custom_call_target="tpu_custom_call" | custom-call | tf_op jit(solution)/shard_map/mega/pallas_call | solution.py:781
  76.5 1.3 %reshape.19 = f32[768]{0:T(1024)} reshape(f32[2,384]{1,0:T(2,128)} %get-tuple-element.8) | data formatting | bytes 6144 | tf_op jit(solution)/shard_map/reshape | solution.py:805
  77.7 1.6 %copy.14 = f32[64,512]{1,0:T(8,128)} copy(f32[64,512]{1,0:T(8,128)} %get-tuple-element.17) | data formatting | bytes 262144
  79.3 1.4 %copy.15 = f32[128,64]{0,1:T(8,128)} copy(f32[128,64]{0,1:T(8,128)} %bitcast.2) | data formatting | bytes 65536
  80.7 1.9 %copy.16 = f32[256,512]{1,0:T(8,128)} copy(f32[256,512]{1,0:T(8,128)} %get-tuple-element.19) | data formatting | bytes 1048576

commit v2 on v1

--- a/solution.py
+++ b/solution.py
@@ -252,13 +252,14 @@
         and s.wshare % 16 == 0
         and s.N % 2 == 0
         and s.X * s.Z == s.P
+        and s.Z == 4
     )
 
 
 def scratch_of(s):
     U, H, D, lw, I, N, Y, X, Z = s.U, s.H, s.D, s.lw, s.I, s.N, s.Y, s.X, s.Z
     lh, share, tshare, wshare, CH = lw // HEAD, s.share, s.tshare, s.wshare, s.CH
-    X1, Z1, Y1 = max(X - 1, 1), max(Z - 1, 1), max(Y - 1, 1)
+    X1, Y1 = max(X - 1, 1), max(Y - 1, 1)
     V = pltpu.VMEM
     return dict(
         item_v=V((I, D), bf16),
@@ -282,9 +283,7 @@
         hot=V((U * H, I), bf16),
         tid_col=V((U, H, LANES), f32),
         counts=V((I // CH, 1, CH), f32),
-        tgt=V((U, H, D), f32),
         acc=V((U, H, D), f32),
-        nacc=V((H, LANES), f32),
         zst=V((U, N, 8, H), f32),
         up=V((U, Y, share, D), bf16),
         r1=V((U, Y, share, D), bf16),
@@ -299,20 +298,22 @@
         row_send=V((Z, X1, D, tshare), bf16),
         row_own=V((Z, D, tshare), f32),
         row_rx=V((Z, X1, D, tshare), bf16),
-        row_zs=V((Z1, D, tshare), bf16),
-        row_rz=V((Z1, D, tshare), bf16),
+        row_zs=V((Z, D, tshare), bf16),
+        row_rz=V((Z, D, tshare), bf16),
         g_acc=V((D, 5 * lw), f32),
         g_send=V((Z, X1, wshare, 5 * lw), bf16),
         g_rx=V((Z, X1, wshare, 5 * lw), bf16),
-        g_zs=V((Z1, wshare, 5 * lw), bf16),
-        g_rz=V((Z1, wshare, 5 * lw), bf16),
-        item_sem=pltpu.SemaphoreType.DMA(()),
+        g_zs=V((Z, wshare, 5 * lw), bf16),
+        g_rz=V((Z, wshare, 5 * lw), bf16),
+        hist=V((U, H, D), bf16),
+        w_in=V((D, 4 * lw), bf16),
+        in_sem=pltpu.SemaphoreType.DMA((U + 3,)),
         ssem=pltpu.SemaphoreType.DMA((192,)),
         rsem=pltpu.SemaphoreType.DMA((192,)),
     )
 
 
-def mega(s, names, hist_ref, len_ref, w_in_ref, w_out_ref, tid_ref, nid_ref, item_hbm,
+def mega(s, names, hist_hbm, len_ref, w_in_hbm, w_out_hbm, tid_ref, nid_ref, item_hbm,
          loss_ref, gwin_ref, gwout_ref, gtab_ref, *scratch):
     R = SimpleNamespace(**dict(zip(names, scratch)))
     U, H, D, lw, I, N, Y, X, Z = s.U, s.H, s.D, s.lw, s.I, s.N, s.Y, s.X, s.Z
@@ -331,8 +332,18 @@
 
     neg_peers = [turn(n, k, N) for k in range(1, N)]
     x_peers = [(z * X + turn(x, k, X), n) for k in range(1, X)]
-    z_peers = [(turn(z, k, Z) * X + x, n) for k in range(1, Z)]
-    everyone = [at_neg(p) for p in neg_peers] + x_peers + z_peers
+
+    def flip(index, bits):
+        bit = 1
+        while bit <= bits:
+            if bits & bit:
+                index = index + bit - 2 * bit * lax.rem(lax.div(index, bit), 2)
+            bit *= 2
+        return index
+
+    levels = [1 << k for k in range(Z.bit_length() - 1)]
+    z_peers = {bit: (flip(z, bit) * X + x, n) for bit in levels}
+    everyone = [at_neg(p) for p in neg_peers] + x_peers + list(z_peers.values())
 
     barrier = pltpu.get_barrier_semaphore()
     for peer in everyone:
@@ -354,10 +365,19 @@
         sent.append(copy)
         return copy
 
-    item_copy = pltpu.make_async_copy(item_hbm, R.item_v, R.item_sem)
+    loads = [(w_in_hbm, R.w_in), (w_out_hbm, R.wout_all.at[n])]
+    loads += [(hist_hbm.at[pl.ds(b * H, H)], R.hist.at[b]) for b in range(U)]
+    loads += [(item_hbm, R.item_v)]
+    loads = [pltpu.make_async_copy(a, c, R.in_sem.at[i]) for i, (a, c) in enumerate(loads)]
+    w_in_load, w_out_load, hist_loads, item_copy = loads[0], loads[1], loads[2 : 2 + U], loads[2 + U]
+    w_in_load.start()
+    for copy in hist_loads:
+        copy.start()
+    w_out_load.start()
     item_copy.start()
 
-    w_in = w_in_ref[...]
+    w_in_load.wait()
+    w_in = R.w_in[...]
     pieces = []
     for part in range(4):
         for h in range(lh):
@@ -377,7 +397,8 @@
         return R.proj[b, :, part * lw : (part + 1) * lw]
 
     def project(b):
-        rows = hist_ref[b * H : (b + 1) * H, :].astype(f32)
+        hist_loads[b].wait()
+        rows = R.hist[b].astype(f32)
         normed = moment_norm(rows)[0].astype(bf16)
         R.normed[b] = normed
         pre = dot_nn(normed, R.wperm[...])
@@ -430,10 +451,10 @@
         for copy in relays:
             copy.wait_recv()
 
+    pl.semaphore_wait(barrier, len(everyone))
+    w_out_load.wait()
+    wout_state = gather_start(R.wout_all)
     project(0)
-    pl.semaphore_wait(barrier, len(everyone))
-    R.wout_all[n] = w_out_ref[...]
-    wout_state = gather_start(R.wout_all)
     attend(0)
     stat_copies = [send_stats(0)]
     project(1)
@@ -455,7 +476,8 @@
     lax.fori_loop(0, I // step_rows, norm_items, 0)
 
     gather_states = []
-    for b in range(U):
+
+    def mix(b):
         for copy in stat_copies[b]:
             copy.wait_recv()
         total = R.stat[b, 0]
@@ -469,10 +491,8 @@
         R.att[b] = centred
         R.mixed_all[b, n] = (centred * part_of(b, 0).astype(f32)).astype(bf16)
         gather_states.append(gather_start(R.mixed_all.at[b]))
-    gate_copies = [send_gates(b) for b in range(U)]
-    for b in range(U):
-        R.gate_rows[b, n] = R.proj[b, pl.ds(pl.multiple_of(n * share, 16), share), 0:lw]
-
+
+    mix(0)
     slots = nid_ref[...] - n * I
     high = lax.shift_right_logical(slots, 7)
     low = lax.bitwise_and(slots, LANES - 1)
@@ -489,113 +509,105 @@
             [table[i * groups + g : i * groups + g + 1, :] for g in range(groups)], axis=1
         )
 
+    for b in range(U):
+        ids = (tid_ref[b * H : (b + 1) * H].reshape(1, H) - n * I).astype(f32)
+        R.tid_col[b] = jnp.broadcast_to(ids, (LANES, H)).T
+
+    for b in range(1, U):
+        mix(b)
+    gate_copies = [send_gates(b) for b in range(U)]
+    for b in range(U):
+        R.gate_rows[b, n] = R.proj[b, pl.ds(pl.multiple_of(n * share, 16), share), 0:lw]
+
     def is_target(b, i):
         ids = jnp.concatenate([R.tid_col[b]] * groups, axis=1)
         place = lax.broadcasted_iota(jnp.int32, (H, CH), 1) + i * CH
         return ids == place.astype(f32)
 
-    def targets(b):
-        ids = (tid_ref[b : b + 1, :] - n * I).astype(f32)
-        R.tid_col[b] = jnp.broadcast_to(ids, (LANES, H)).T
-        R.tgt[b] = jnp.zeros((H, D), f32)
-
-        def body(i, carry):
-            cols = pl.ds(pl.multiple_of(i * CH, CH), CH)
-            hot = jnp.where(is_target(b, i), 1.0, 0.0).astype(bf16)
-            R.hot[b * H : (b + 1) * H, cols] = hot
-            R.tgt[b] += dot_nn(hot, R.item_r[cols, :])
-            return carry
-
-        lax.fori_loop(0, I // CH, body, 0)
+    def target_rows(b):
+        return dot_nn(R.hot[b * H : (b + 1) * H, :], R.item_r[...])
 
     wout_relays = gather_relay(R.wout_all, wout_state)
-    targets(0)
-    relays = [gather_relay(R.mixed_all.at[0], gather_states[0])]
-    for b in range(1, U):
-        targets(b)
-        relays.append(gather_relay(R.mixed_all.at[b], gather_states[b]))
-
     for b in range(U):
         R.normed_t[:, b * H : (b + 1) * H] = R.normed[b].astype(f32).T.astype(bf16)
+
+    def prepare_backward(b):
         mask = attn_mask(b)
         for h in range(lh):
             R.scores[b, h] = silu_grad(R.scores[b, h]) * mask
 
+    relays = [gather_relay(R.mixed_all.at[0], gather_states[0])]
     gather_wait(wout_state, wout_relays)
     z_copies = []
     for b in range(U):
         gather_wait(gather_states[b], relays[b])
         mixed = jnp.concatenate([R.mixed_all[b, d] for d in range(N)], axis=1)
         w_out_full = R.wout_all[...].reshape(N * lw, D)
-        output = hist_ref[b * H : (b + 1) * H, :].astype(f32) + dot_nn(mixed, w_out_full)
+        output = R.hist[b].astype(f32) + dot_nn(mixed, w_out_full)
         R.out[b] = output
         unit = normalize_rows(output)[0].astype(bf16)
         scaled = unit * jnp.asarray(logit_scale, bf16)
         R.u64[b] = scaled
-        positive = jnp.sum(scaled.astype(f32) * R.tgt[b], -1, keepdims=True)
-        R.acc[b] = jnp.zeros((H, D), f32)
-        R.nacc[...] = jnp.zeros((H, LANES), f32)
-
-        def body(i, carry, b=b):
-            cols = pl.ds(pl.multiple_of(i * CH, CH), CH)
-            items = R.item_r[cols, :]
-            terms = jnp.exp(dot_nt(R.u64[b], items)) * R.counts[i]
-            terms = jnp.where(is_target(b, i), 0.0, terms)
-            partial = terms[:, 0:LANES]
-            for g in range(1, groups):
+        if b + 1 < U:
+            relays.append(gather_relay(R.mixed_all.at[b + 1], gather_states[b + 1]))
+        partial, picked = jnp.zeros((H, LANES), f32), jnp.zeros((H, LANES), f32)
+        for i in range(I // CH):
+            cols = slice(i * CH, (i + 1) * CH)
+            logits = dot_nt(scaled, R.item_r[cols, :])
+            target = is_target(b, i)
+            terms = jnp.where(target, 0.0, jnp.exp(logits) * R.counts[i])
+            chosen = jnp.where(target, logits, 0.0)
+            for g in range(groups):
                 partial = partial + terms[:, g * LANES : (g + 1) * LANES]
-            R.nacc[...] += partial
-            half = terms.astype(bf16)
-            R.exps[b * H : (b + 1) * H, cols] = half
-            R.acc[b] += dot_nn(half, items)
-            return carry
-
-        lax.fori_loop(0, I // CH, body, 0)
-        negative = jnp.sum(R.nacc[...], -1, keepdims=True)
+                picked = picked + chosen[:, g * LANES : (g + 1) * LANES]
+            R.hot[b * H : (b + 1) * H, cols] = jnp.where(target, 1.0, 0.0).astype(bf16)
+            R.exps[b * H : (b + 1) * H, cols] = terms.astype(bf16)
+        negative = jnp.sum(partial, -1, keepdims=True)
+        positive = jnp.sum(picked, -1, keepdims=True)
         R.zst[b, n] = columns_to_rows([negative, positive])
         z_copies.append([send(R.zst.at[b, n], R.zst.at[b, n], at_neg(p)) for p in neg_peers])
 
-    r1_copies = []
-    for b in range(U):
+        R.acc[b] = dot_nn(R.exps[b * H : (b + 1) * H, :], R.item_r[...])
+
+    r1_copies, r2_copies = [None] * U, [None] * U
+
+    def share_rows(owner):
+        return pl.ds(pl.multiple_of(owner * share, 8), share)
+
+    def partition(b):
         for copy in z_copies[b]:
             copy.wait_recv()
         total = R.zst[b, 0]
         for d in range(1, N):
             total = total + R.zst[b, d]
         negative, positive = total[0:1], total[1:2]
-        partition = jnp.exp(positive) + negative
+        whole = jnp.exp(positive) + negative
         live = lax.broadcasted_iota(jnp.int32, (1, H), 1) < len_ref[b]
-        loss_ref[b : b + 1, :] = jnp.where(live, jnp.log(partition) - positive, 0.0)
-        factor = jnp.where(live, 1.0 / partition, 0.0)
-        columns = rows_to_columns([factor, -negative])
-        factor_col, negative_col = columns[:, 0:1], columns[:, 1:2]
-        unit_part = (logit_scale * factor_col) * (R.acc[b] + negative_col * R.tgt[b])
-        R.acc[b] = unit_part
-        copies = []
-        for other in range(Y):
-            first = pl.multiple_of((other * 2 + (1 - core)) * share, 8)
-            R.up[b, other] = R.acc[b, pl.ds(first, share), :].astype(bf16)
-            copies.append(send(R.up.at[b, other], R.r1.at[b, other], at_neg(partner)))
-        r1_copies.append(copies)
+        loss_ref[:, b * H : (b + 1) * H] = jnp.where(live, jnp.log(whole) - positive, 0.0)
+        columns = rows_to_columns([jnp.where(live, 1.0 / whole, 0.0), -negative])
+        return columns[:, 0:1], columns[:, 1:2]
+
+    def coefficients(b, factor_col, negative_col):
         scaled_rows = R.u64[b].astype(f32) * factor_col
         R.ru_t[:, b * H : (b + 1) * H] = scaled_rows.T.astype(bf16)
         negative_half = negative_col.astype(bf16)
 
-        def fix(i, carry, b=b, negative_half=negative_half):
+        def fix(i, carry):
             cols = pl.ds(pl.multiple_of(i * CH, CH), CH)
-            R.exps[b * H : (b + 1) * H, cols] += (
-                R.hot[b * H : (b + 1) * H, cols] * negative_half
-            )
+            R.exps[b * H : (b + 1) * H, cols] += R.hot[b * H : (b + 1) * H, cols] * negative_half
             return carry
 
         lax.fori_loop(0, I // CH, fix, 0)
 
-    r2_copies = []
-
-    def share_rows(owner):
-        return pl.ds(pl.multiple_of(owner * share, 8), share)
-
-    for b in range(U):
+    def unit_send(b, factor_col, negative_col, target):
+        R.acc[b] = (logit_scale * factor_col) * (R.acc[b] + negative_col * target)
+        copies = []
+        for other in range(Y):
+            R.up[b, other] = R.acc[b, share_rows(other * 2 + (1 - core)), :].astype(bf16)
+            copies.append(send(R.up.at[b, other], R.r1.at[b, other], at_neg(partner)))
+        r1_copies[b] = copies
+
+    def unit_relay(b):
         for copy in r1_copies[b]:
             copy.wait_recv()
         copies = []
@@ -605,23 +617,53 @@
                 R.acc[b, share_rows(other * 2 + core), :] + R.r1[b, other].astype(f32)
             ).astype(bf16)
             copies.append(send(R.s2.at[b, k - 1], R.r2.at[b, k - 1], at_neg(other * 2 + core)))
-        r2_copies.append(copies)
+        r2_copies[b] = copies
 
     def row_block(index):
         cols = pl.ds(pl.multiple_of(index * tshare, LANES), tshare)
         return dot_nn(R.ru_t[...], R.exps[:, cols])
 
-    z_order = list(range(1, Z)) + [0]
-    row_x = dict()
-    for kz in z_order:
+    z_order = list(range(Z - 1, -1, -1))
+    row_x, g_x = dict(), dict()
+
+    def row_compute(r):
         for kx in range(1, X):
-            target = turn(z, kz, Z) * X + turn(x, kx, X)
-            R.row_send[kz, kx - 1] = row_block(target).astype(bf16)
-            row_x[kz, kx] = send(
-                R.row_send.at[kz, kx - 1], R.row_rx.at[kz, kx - 1], x_peers[kx - 1]
-            )
-
-    mg_copies, og_copies = [], []
+            R.row_send[r, kx - 1] = row_block(flip(z, r) * X + turn(x, kx, X)).astype(bf16)
+
+    def row_start(r):
+        row_x[r] = [
+            send(R.row_send.at[r, kx - 1], R.row_rx.at[r, kx - 1], x_peers[kx - 1])
+            for kx in range(1, X)
+        ]
+
+    for b in range(U):
+        if b == U - 1:
+            columns = partition(b)
+            coefficients(b, *columns)
+            row_compute(z_order[0])
+            row_start(z_order[0])
+            if b > 0:
+                unit_relay(b - 1)
+            unit_send(b, *columns, target_rows(b))
+        else:
+            columns = partition(b)
+            coefficients(b, *columns)
+            unit_send(b, *columns, target_rows(b))
+            if b > 0:
+                unit_relay(b - 1)
+    row_compute(z_order[1])
+    unit_relay(U - 1)
+    for r in z_order[2:]:
+        row_compute(r)
+    for b in range(U):
+        prepare_backward(b)
+    for r in z_order:
+        R.row_own[r] = row_block(flip(z, r) * X + x)
+
+    for copies in gate_copies:
+        for copy in copies:
+            copy.wait_recv()
+    mg_copies = []
     for b in range(U):
         for copy in r2_copies[b]:
             copy.wait_recv()
@@ -636,10 +678,6 @@
         for d in range(N):
             mixed_grad = dot_nt(half, R.wout_all[d])
             R.mg_send[b, d] = mixed_grad.astype(bf16)
-            if b == 0 and d == 0:
-                for copies in gate_copies:
-                    for copy in copies:
-                        copy.wait_recv()
             sum_g = sum_g + jnp.sum(mixed_grad * R.gate_rows[b, d].astype(f32), -1, keepdims=True)
             mixed = R.mixed_all[b, d, share_rows(n), :].astype(f32)
             sum_gc = sum_gc + jnp.sum(mixed_grad * mixed, -1, keepdims=True)
@@ -656,24 +694,29 @@
             copies.append(send(R.mg_send.at[b, p], R.mg_recv.at[b, n], at_neg(p)))
             copies.append(send(R.bs_send.at[b], R.bs_recv.at[b, n], at_neg(p)))
         mg_copies.append(copies)
-    for b in range(U):
-        og_copies.append([send(R.og_all.at[b, n], R.og_all.at[b, n], at_neg(p)) for p in neg_peers])
-
-    for kz in z_order:
-        R.row_own[kz] = row_block(turn(z, kz, Z) * X + x)
-
-    row_z = []
-
-    def row_forward(kz):
-        block = R.row_own[kz]
+        if b == 0:
+            row_start(z_order[1])
+    og_states = [gather_start(R.og_all.at[b]) for b in range(U)]
+
+    def reduce_along_z(r, block, send_ref, recv_ref, slots):
+        step = r & -r if r else Z
+        for bit in levels:
+            if bit < step:
+                slots[r ^ bit].wait_recv()
+                block = block + recv_ref[r ^ bit].astype(f32)
+        if r:
+            send_ref[r] = block.astype(bf16)
+            slots[r] = send(send_ref.at[r], recv_ref.at[r], z_peers[step])
+        return block
+
+    row_z, g_z = dict(), dict()
+
+    def row_forward(r):
+        block = R.row_own[r]
         for kx in range(1, X):
-            row_x[kz, kx].wait_recv()
-            block = block + R.row_rx[kz, kx - 1].astype(f32)
-        if kz == 0:
-            R.row_own[0] = block
-        else:
-            R.row_zs[kz - 1] = block.astype(bf16)
-            row_z.append(send(R.row_zs.at[kz - 1], R.row_rz.at[kz - 1], z_peers[kz - 1]))
+            row_x[r][kx - 1].wait_recv()
+            block = block + R.row_rx[r, kx - 1].astype(f32)
+        return reduce_along_z(r, block, R.row_zs, R.row_rz, row_z)
 
     def backward(b):
         for copy in mg_copies[b]:
@@ -710,53 +753,35 @@
 
     row_forward(z_order[0])
     backward(0)
-    if Z > 1:
-        row_forward(z_order[1])
+    row_start(z_order[2])
+    og_relays = [gather_relay(R.og_all.at[b], og_states[b]) for b in range(U)]
     for b in range(1, U):
         backward(b)
+    row_forward(z_order[1])
     grad_out = jnp.zeros((lw, D), f32)
     for b in range(U):
-        for copy in og_copies[b]:
-            copy.wait_recv()
+        gather_wait(og_states[b], og_relays[b])
         grad_out = grad_out + dot_tn(R.mixed_all[b, n], R.og_all[b].reshape(H, D))
     R.g_acc[:, 4 * lw : 5 * lw] = grad_out.T
 
     def g_rows(index):
         return R.g_acc[pl.ds(pl.multiple_of(index * wshare, 8), wshare), :]
 
-    g_x, g_z = dict(), []
-    for kz in z_order:
+    for r in z_order:
         for kx in range(1, X):
-            target = turn(z, kz, Z) * X + turn(x, kx, X)
-            R.g_send[kz, kx - 1] = g_rows(target).astype(bf16)
-            g_x[kz, kx] = send(R.g_send.at[kz, kx - 1], R.g_rx.at[kz, kx - 1], x_peers[kx - 1])
-    for kz in z_order[2:]:
-        row_forward(kz)
-    own_g = None
-    for kz in z_order:
-        block = g_rows(turn(z, kz, Z) * X + x)
+            R.g_send[r, kx - 1] = g_rows(flip(z, r) * X + turn(x, kx, X)).astype(bf16)
+        g_x[r] = [
+            send(R.g_send.at[r, kx - 1], R.g_rx.at[r, kx - 1], x_peers[kx - 1])
+            for kx in range(1, X)
+        ]
+    row_start(z_order[3])
+    row_forward(z_order[2])
+    for r in z_order:
+        block = g_rows(flip(z, r) * X + x)
         for kx in range(1, X):
-            g_x[kz, kx].wait_recv()
-            block = block + R.g_rx[kz, kx - 1].astype(f32)
-        if kz == 0:
-            own_g = block
-        else:
-            R.g_zs[kz - 1] = block.astype(bf16)
-            g_z.append(send(R.g_zs.at[kz - 1], R.g_rz.at[kz - 1], z_peers[kz - 1]))
-
-    for copy in row_z:
-        copy.wait_recv()
-    row_total = R.row_own[0]
-    for k in range(Z - 1):
-        row_total = row_total + R.row_rz[k].astype(f32)
-    own_items = R.item_v[pl.ds(pl.multiple_of(me_dp * tshare, 16), tshare), :].astype(f32)
-    unit, inverse = normalize_rows(own_items)
-    gtab_ref[...] = project_rows(row_total.T, unit, inverse)
-
-    for copy in g_z:
-        copy.wait_recv()
-    for k in range(Z - 1):
-        own_g = own_g + R.g_rz[k].astype(f32)
+            g_x[r][kx - 1].wait_recv()
+            block = block + R.g_rx[r, kx - 1].astype(f32)
+        own_g = reduce_along_z(r, block, R.g_zs, R.g_rz, g_z)
     pieces = []
     for h in range(lh):
         for part in range(4):
@@ -764,8 +789,19 @@
             pieces.append(own_g[:, first : first + HEAD])
     gwin_ref[...] = jnp.concatenate(pieces, axis=1)
     gwout_ref[...] = own_g[:, 4 * lw : 5 * lw]
+    row_total = row_forward(0)
+    own_items = R.item_v[pl.ds(pl.multiple_of(me_dp * tshare, 16), tshare), :].astype(f32)
+    unit, inverse = normalize_rows(own_items)
+    gtab_ref[...] = project_rows(row_total.T, unit, inverse)
     for copy in sent:
         copy.wait_send()
+
+
+def finish(loss_in, gwin_in, gwout_in, gtab_in, loss_ref, gwin_ref, gwout_ref, gtab_ref):
+    loss_ref[...] = loss_in[...].reshape(loss_ref.shape)
+    gwin_ref[...] = gwin_in[...]
+    gwout_ref[...] = gwout_in[...]
+    gtab_ref[...] = gtab_in[...]
 
 
 def on_device(dp_size, neg_size, history, lengths, w_in, w_out, target_ids, negative_ids, item_table):
@@ -777,16 +813,17 @@
     scratch = scratch_of(s)
     vmem = pl.BlockSpec(memory_space=pltpu.VMEM)
     smem = pl.BlockSpec(memory_space=pltpu.SMEM)
+    hbm = pl.BlockSpec(memory_space=pl.ANY)
     U, H, D, lw = s.U, s.H, s.D, s.lw
     loss, grad_in, grad_out, grad_table = pl.pallas_call(
         functools.partial(mega, s, tuple(scratch)),
         out_shape=(
-            jax.ShapeDtypeStruct((U, H), f32),
+            jax.ShapeDtypeStruct((1, U * H), f32),
             jax.ShapeDtypeStruct((s.wshare, 4 * lw), f32),
             jax.ShapeDtypeStruct((s.wshare, lw), f32),
             jax.ShapeDtypeStruct((s.tshare, D), f32),
         ),
-        in_specs=[vmem, smem, vmem, vmem, vmem, vmem, pl.BlockSpec(memory_space=pl.ANY)],
+        in_specs=[hbm, smem, hbm, hbm, vmem, vmem, hbm],
         out_specs=(vmem, vmem, vmem, vmem),
         scratch_shapes=list(scratch.values()),
         compiler_params=pltpu.CompilerParams(
@@ -798,11 +835,23 @@
         lengths,
         w_in,
         w_out,
-        target_ids.reshape(U, H),
+        target_ids,
         negative_ids.reshape(1, s.NB),
         item_table,
     )
-    return (loss.reshape(U * H), grad_in, grad_out.T, grad_table)
+    loss, grad_in, grad_out, grad_table = pl.pallas_call(
+        finish,
+        out_shape=(
+            jax.ShapeDtypeStruct((U * H,), f32),
+            jax.ShapeDtypeStruct((s.wshare, 4 * lw), f32),
+            jax.ShapeDtypeStruct((s.wshare, lw), f32),
+            jax.ShapeDtypeStruct((s.tshare, D), f32),
+        ),
+        in_specs=[vmem] * 4,
+        out_specs=(vmem,) * 4,
+        name="finish",
+    )(loss, grad_in, grad_out, grad_table)
+    return (loss, grad_in, grad_out.T, grad_table)
 
 
 def solution(mesh):

time: 82.9 us -> 72.8 us (0.88)
  local copies, waits for them, and re-layouts: 7.35 us -> 0 us
  Pallas kernels: 74.6 us -> 71.3 us
    pallas_call x1, Pallas kernels: 74.6 us -> 69.3 us  [on_device(): pl.pallas_call(functools.partial(mega, s, tuple(scratch)), out_shape=(jax...]
    unnamed x3 -> x0, local copies, waits for them, and re-layouts: 4.81 us -> none
    reshape x2 -> x0, local copies, waits for them, and re-layouts: 2.55 us -> none  [the longest x1 1.27 us: on_device(): return (loss.reshape(U * H), grad_in, grad_out.T, grad_table)]
    pallas_call x0 -> x1, Pallas kernels: none -> 2 us  [on_device(): pl.pallas_call(finish, out_shape=(jax.ShapeDtypeStruct((U * H,), f32), ja...]
where the time goes in v2:
time: 72.8 us; the launch traced here: 71.9 us
  Pallas kernels  71.3 us (98%)
    pallas_call x1, Pallas kernels, on_device(): pl.pallas_call(functools.partial(mega, s, tuple(scratch)), out_shape=(jax...  69.3 us
    pallas_call x1, Pallas kernels, on_device(): pl.pallas_call(finish, out_shape=(jax.ShapeDtypeStruct((U * H,), f32), ja...  2 us

profile of v2, /device:TPU:0, one launch (start us, length us, event | category | flops | bytes accessed | tf_op | source)
XLA Modules:
  0.0 71.9 jit_solution(11182429849653735714)
XLA Ops:
  0.6 69.3 %mega.1 = (f32[1,768]{1,0:T(1,128)}, f32[64,512]{1,0:T(8,128)}, f32[64,128]{1,0:T(8,128)}, f32[256,512]{1,0:T(8,128)}) custom-call(bf16[768,512]{1,0:T(8,128)(2,1)} %hist_hbm.1, s32[2]{0:T(128)} %len_ref.1, bf16[512,512]{1,0:T(8,128)(2,1)} %w_in_hbm.1, bf16[128,512]{1,0:T(8,128)(2,1)} %w_out_hbm.1, s32[768]{0:T(1024)} %tid_ref.1, s32[1,4096]{1,0:T(1,128)} %bitcast.2, ...), custom_call_target="tpu_custom_call" | custom-call | tf_op jit(solution)/shard_map/mega/pallas_call | solution.py:818
  69.9 2.0 %finish.1 = (f32[768]{0:T(1024)}, f32[64,512]{1,0:T(8,128)}, f32[64,128]{1,0:T(8,128)}, f32[256,512]{1,0:T(8,128)}) custom-call(f32[1,768]{1,0:T(1,128)} %get-tuple-element.12.loss_in, f32[64,512]{1,0:T(8,128)} %get-tuple-element.13.gwin_in, f32[64,128]{1,0:T(8,128)} %get-tuple-element.14.gwout_in, f32[256,512]{1,0:T(8,128)} %get-tuple-element.15.gtab_in), custom_call_target="tpu_custom_call" | custom-call | tf_op jit(solution)/shard_map/finish/pallas_call | solution.py:842

commit v3 on v2

--- a/solution.py
+++ b/solution.py
@@ -237,6 +237,7 @@
     s.tshare = s.I // dp_size
     s.wshare = s.D // dp_size
     s.CH = 4 * LANES
+    s.q = s.D // 4
     return s
 
 
@@ -253,12 +254,13 @@
         and s.N % 2 == 0
         and s.X * s.Z == s.P
         and s.Z == 4
+        and s.q % 16 == 0
     )
 
 
 def scratch_of(s):
     U, H, D, lw, I, N, Y, X, Z = s.U, s.H, s.D, s.lw, s.I, s.N, s.Y, s.X, s.Z
-    lh, share, tshare, wshare, CH = lw // HEAD, s.share, s.tshare, s.wshare, s.CH
+    lh, share, tshare, wshare, CH, q = lw // HEAD, s.share, s.tshare, s.wshare, s.CH, s.q
     X1, Y1 = max(X - 1, 1), max(Y - 1, 1)
     V = pltpu.VMEM
     return dict(
@@ -295,11 +297,16 @@
         bs_send=V((U, 8, LANES), f32),
         bs_recv=V((U, N, 8, LANES), f32),
         ru_t=V((D, U * H), bf16),
-        row_send=V((Z, X1, D, tshare), bf16),
-        row_own=V((Z, D, tshare), f32),
-        row_rx=V((Z, X1, D, tshare), bf16),
-        row_zs=V((Z, D, tshare), bf16),
-        row_rz=V((Z, D, tshare), bf16),
+        row_send=V((Z, X1, D - q, tshare), bf16),
+        row_own=V((Z, D - q, tshare), f32),
+        row_rx=V((Z, X1, D - q, tshare), bf16),
+        row_zs=V((Z, D - q, tshare), bf16),
+        row_rz=V((Z, D - q, tshare), bf16),
+        zf_own=V((X, q, tshare), f32),
+        zf_zs=V((Z, X, q, tshare), bf16),
+        zf_rz=V((Z, X, q, tshare), bf16),
+        zf_send=V((X1, q, tshare), bf16),
+        zf_rx=V((X1, q, tshare), bf16),
         g_acc=V((D, 5 * lw), f32),
         g_send=V((Z, X1, wshare, 5 * lw), bf16),
         g_rx=V((Z, X1, wshare, 5 * lw), bf16),
@@ -307,17 +314,20 @@
         g_rz=V((Z, wshare, 5 * lw), bf16),
         hist=V((U, H, D), bf16),
         w_in=V((D, 4 * lw), bf16),
-        in_sem=pltpu.SemaphoreType.DMA((U + 3,)),
+        tid=V((U * H,), jnp.int32),
+        nid=V((s.NB,), jnp.int32),
+        length=pltpu.SMEM((U,), jnp.int32),
+        in_sem=pltpu.SemaphoreType.DMA((U + 6,)),
         ssem=pltpu.SemaphoreType.DMA((192,)),
         rsem=pltpu.SemaphoreType.DMA((192,)),
     )
 
 
-def mega(s, names, hist_hbm, len_ref, w_in_hbm, w_out_hbm, tid_ref, nid_ref, item_hbm,
+def mega(s, names, hist_hbm, len_hbm, w_in_hbm, w_out_hbm, tid_hbm, nid_hbm, item_hbm,
          loss_ref, gwin_ref, gwout_ref, gtab_ref, *scratch):
     R = SimpleNamespace(**dict(zip(names, scratch)))
     U, H, D, lw, I, N, Y, X, Z = s.U, s.H, s.D, s.lw, s.I, s.N, s.Y, s.X, s.Z
-    lh, share, tshare, wshare, CH = lw // HEAD, s.share, s.tshare, s.wshare, s.CH
+    lh, share, tshare, wshare, CH, q = lw // HEAD, s.share, s.tshare, s.wshare, s.CH, s.q
     me_dp = lax.axis_index("dp")
     n = lax.axis_index("neg")
     y, core = lax.div(n, 2), lax.rem(n, 2)
@@ -367,14 +377,15 @@
 
     loads = [(w_in_hbm, R.w_in), (w_out_hbm, R.wout_all.at[n])]
     loads += [(hist_hbm.at[pl.ds(b * H, H)], R.hist.at[b]) for b in range(U)]
-    loads += [(item_hbm, R.item_v)]
+    loads += [(item_hbm, R.item_v), (tid_hbm, R.tid), (nid_hbm, R.nid), (len_hbm, R.length)]
     loads = [pltpu.make_async_copy(a, c, R.in_sem.at[i]) for i, (a, c) in enumerate(loads)]
     w_in_load, w_out_load, hist_loads, item_copy = loads[0], loads[1], loads[2 : 2 + U], loads[2 + U]
     w_in_load.start()
     for copy in hist_loads:
         copy.start()
     w_out_load.start()
-    item_copy.start()
+    for copy in loads[3 + U :]:
+        copy.start()
 
     w_in_load.wait()
     w_in = R.w_in[...]
@@ -384,6 +395,8 @@
             first = (h * 4 + part) * HEAD
             pieces.append(w_in[:, first : first + HEAD])
     R.wperm[...] = jnp.concatenate(pieces, axis=1)
+    item_copy.start()
+    loads[5 + U].wait()
 
     head_lane = lax.div(lax.broadcasted_iota(jnp.int32, (1, lw), 1), HEAD)
     head_mask = [jnp.where(head_lane == h, 1.0, 0.0).astype(bf16) for h in range(lh)]
@@ -391,7 +404,7 @@
     def attn_mask(b):
         row = lax.broadcasted_iota(jnp.int32, (H, H), 0)
         col = lax.broadcasted_iota(jnp.int32, (H, H), 1)
-        return jnp.where((col <= row) & (row < len_ref[b]), 1.0 / H, 0.0)
+        return jnp.where((col <= row) & (row < R.length[b]), 1.0 / H, 0.0)
 
     def part_of(b, part):
         return R.proj[b, :, part * lw : (part + 1) * lw]
@@ -493,7 +506,9 @@
         gather_states.append(gather_start(R.mixed_all.at[b]))
 
     mix(0)
-    slots = nid_ref[...] - n * I
+    loads[3 + U].wait()
+    loads[4 + U].wait()
+    slots = R.nid[...].reshape(1, s.NB) - n * I
     high = lax.shift_right_logical(slots, 7)
     low = lax.bitwise_and(slots, LANES - 1)
     coarse = jnp.where(
@@ -510,7 +525,7 @@
         )
 
     for b in range(U):
-        ids = (tid_ref[b * H : (b + 1) * H].reshape(1, H) - n * I).astype(f32)
+        ids = (R.tid[b * H : (b + 1) * H].reshape(1, H) - n * I).astype(f32)
         R.tid_col[b] = jnp.broadcast_to(ids, (LANES, H)).T
 
     for b in range(1, U):
@@ -523,9 +538,6 @@
         ids = jnp.concatenate([R.tid_col[b]] * groups, axis=1)
         place = lax.broadcasted_iota(jnp.int32, (H, CH), 1) + i * CH
         return ids == place.astype(f32)
-
-    def target_rows(b):
-        return dot_nn(R.hot[b * H : (b + 1) * H, :], R.item_r[...])
 
     wout_relays = gather_relay(R.wout_all, wout_state)
     for b in range(U):
@@ -567,7 +579,6 @@
         R.zst[b, n] = columns_to_rows([negative, positive])
         z_copies.append([send(R.zst.at[b, n], R.zst.at[b, n], at_neg(p)) for p in neg_peers])
 
-        R.acc[b] = dot_nn(R.exps[b * H : (b + 1) * H, :], R.item_r[...])
 
     r1_copies, r2_copies = [None] * U, [None] * U
 
@@ -582,7 +593,7 @@
             total = total + R.zst[b, d]
         negative, positive = total[0:1], total[1:2]
         whole = jnp.exp(positive) + negative
-        live = lax.broadcasted_iota(jnp.int32, (1, H), 1) < len_ref[b]
+        live = lax.broadcasted_iota(jnp.int32, (1, H), 1) < R.length[b]
         loss_ref[:, b * H : (b + 1) * H] = jnp.where(live, jnp.log(whole) - positive, 0.0)
         columns = rows_to_columns([jnp.where(live, 1.0 / whole, 0.0), -negative])
         return columns[:, 0:1], columns[:, 1:2]
@@ -599,8 +610,9 @@
 
         lax.fori_loop(0, I // CH, fix, 0)
 
-    def unit_send(b, factor_col, negative_col, target):
-        R.acc[b] = (logit_scale * factor_col) * (R.acc[b] + negative_col * target)
+    def unit_send(b, factor_col, negative_col):
+        total = dot_nn(R.exps[b * H : (b + 1) * H, :], R.item_r[...])
+        R.acc[b] = (logit_scale * factor_col) * total
         copies = []
         for other in range(Y):
             R.up[b, other] = R.acc[b, share_rows(other * 2 + (1 - core)), :].astype(bf16)
@@ -621,7 +633,7 @@
 
     def row_block(index):
         cols = pl.ds(pl.multiple_of(index * tshare, LANES), tshare)
-        return dot_nn(R.ru_t[...], R.exps[:, cols])
+        return dot_nn(R.ru_t[q:, :], R.exps[:, cols])
 
     z_order = list(range(Z - 1, -1, -1))
     row_x, g_x = dict(), dict()
@@ -636,19 +648,43 @@
             for kx in range(1, X)
         ]
 
+    def reduce_along_z(r, block, send_ref, recv_ref, slots):
+        step = r & -r if r else Z
+        for bit in levels:
+            if bit < step:
+                slots[r ^ bit].wait_recv()
+                block = block + recv_ref[r ^ bit].astype(f32)
+        if r:
+            send_ref[r] = block.astype(bf16)
+            slots[r] = send(send_ref.at[r], recv_ref.at[r], z_peers[step])
+        return block
+
+    row_z, g_z, zf_z = dict(), dict(), dict()
+
+    def zfirst_forward(r):
+        blocks = []
+        for kx in range(X):
+            first = (flip(z, r) * X + turn(x, kx, X)) * tshare
+            cols = pl.ds(pl.multiple_of(first, LANES), tshare)
+            blocks.append(dot_nn(R.ru_t[:q, :], R.exps[:, cols]))
+        return reduce_along_z(r, jnp.stack(blocks), R.zf_zs, R.zf_rz, zf_z)
+
     for b in range(U):
         if b == U - 1:
             columns = partition(b)
             coefficients(b, *columns)
+            for r in z_order:
+                if r % 2 == 1:
+                    zfirst_forward(r)
             row_compute(z_order[0])
             row_start(z_order[0])
             if b > 0:
                 unit_relay(b - 1)
-            unit_send(b, *columns, target_rows(b))
+            unit_send(b, *columns)
         else:
             columns = partition(b)
             coefficients(b, *columns)
-            unit_send(b, *columns, target_rows(b))
+            unit_send(b, *columns)
             if b > 0:
                 unit_relay(b - 1)
     row_compute(z_order[1])
@@ -659,11 +695,13 @@
         prepare_backward(b)
     for r in z_order:
         R.row_own[r] = row_block(flip(z, r) * X + x)
+    row_start(z_order[1])
+    zfirst_forward(2)
 
     for copies in gate_copies:
         for copy in copies:
             copy.wait_recv()
-    mg_copies = []
+    mg_copies, og_states, og_relays = [], [], []
     for b in range(U):
         for copy in r2_copies[b]:
             copy.wait_recv()
@@ -694,22 +732,9 @@
             copies.append(send(R.mg_send.at[b, p], R.mg_recv.at[b, n], at_neg(p)))
             copies.append(send(R.bs_send.at[b], R.bs_recv.at[b, n], at_neg(p)))
         mg_copies.append(copies)
-        if b == 0:
-            row_start(z_order[1])
-    og_states = [gather_start(R.og_all.at[b]) for b in range(U)]
-
-    def reduce_along_z(r, block, send_ref, recv_ref, slots):
-        step = r & -r if r else Z
-        for bit in levels:
-            if bit < step:
-                slots[r ^ bit].wait_recv()
-                block = block + recv_ref[r ^ bit].astype(f32)
-        if r:
-            send_ref[r] = block.astype(bf16)
-            slots[r] = send(send_ref.at[r], recv_ref.at[r], z_peers[step])
-        return block
-
-    row_z, g_z = dict(), dict()
+        og_states.append(gather_start(R.og_all.at[b]))
+    row_start(z_order[2])
+
 
     def row_forward(r):
         block = R.row_own[r]
@@ -753,10 +778,16 @@
 
     row_forward(z_order[0])
     backward(0)
-    row_start(z_order[2])
-    og_relays = [gather_relay(R.og_all.at[b], og_states[b]) for b in range(U)]
+    og_relays.append(gather_relay(R.og_all.at[0], og_states[0]))
     for b in range(1, U):
         backward(b)
+    for b in range(1, U):
+        og_relays.append(gather_relay(R.og_all.at[b], og_states[b]))
+    R.zf_own[...] = zfirst_forward(0)
+    zf_x = []
+    for kx in range(1, X):
+        R.zf_send[kx - 1] = R.zf_own[kx].astype(bf16)
+        zf_x.append(send(R.zf_send.at[kx - 1], R.zf_rx.at[kx - 1], x_peers[kx - 1]))
     row_forward(z_order[1])
     grad_out = jnp.zeros((lw, D), f32)
     for b in range(U):
@@ -789,7 +820,11 @@
             pieces.append(own_g[:, first : first + HEAD])
     gwin_ref[...] = jnp.concatenate(pieces, axis=1)
     gwout_ref[...] = own_g[:, 4 * lw : 5 * lw]
-    row_total = row_forward(0)
+    first_part = R.zf_own[0]
+    for kx in range(1, X):
+        zf_x[kx - 1].wait_recv()
+        first_part = first_part + R.zf_rx[kx - 1].astype(f32)
+    row_total = jnp.concatenate([first_part, row_forward(0)], axis=0)
     own_items = R.item_v[pl.ds(pl.multiple_of(me_dp * tshare, 16), tshare), :].astype(f32)
     unit, inverse = normalize_rows(own_items)
     gtab_ref[...] = project_rows(row_total.T, unit, inverse)
@@ -812,7 +847,6 @@
         )
     scratch = scratch_of(s)
     vmem = pl.BlockSpec(memory_space=pltpu.VMEM)
-    smem = pl.BlockSpec(memory_space=pltpu.SMEM)
     hbm = pl.BlockSpec(memory_space=pl.ANY)
     U, H, D, lw = s.U, s.H, s.D, s.lw
     loss, grad_in, grad_out, grad_table = pl.pallas_call(
@@ -823,7 +857,7 @@
             jax.ShapeDtypeStruct((s.wshare, lw), f32),
             jax.ShapeDtypeStruct((s.tshare, D), f32),
         ),
-        in_specs=[hbm, smem, hbm, hbm, vmem, vmem, hbm],
+        in_specs=[hbm] * 7,
         out_specs=(vmem, vmem, vmem, vmem),
         scratch_shapes=list(scratch.values()),
         compiler_params=pltpu.CompilerParams(
@@ -836,7 +870,7 @@
         w_in,
         w_out,
         target_ids,
-        negative_ids.reshape(1, s.NB),
+        negative_ids,
         item_table,
     )
     loss, grad_in, grad_out, grad_table = pl.pallas_call(

time: 72.8 us -> 64.9 us (0.89)
  Pallas kernels: 71.3 us -> 64.1 us
    pallas_call x1, Pallas kernels: 69.3 us -> 62.1 us  [on_device(): pl.pallas_call(functools.partial(mega, s, tuple(scratch)), out_shape=(jax...]
where the time goes in v3:
time: 64.9 us; the launch traced here: 64.8 us
  Pallas kernels  64.1 us (99%)
    pallas_call x1, Pallas kernels, on_device(): pl.pallas_call(functools.partial(mega, s, tuple(scratch)), out_shape=(jax...  62.1 us
    pallas_call x1, Pallas kernels, on_device(): pl.pallas_call(finish, out_shape=(jax.ShapeDtypeStruct((U * H,), f32), ja...  2 us

profile of v3, /device:TPU:0, one launch (start us, length us, event | category | flops | bytes accessed | tf_op | source)
XLA Modules:
  0.0 64.8 jit_solution(8803018698160163494)
XLA Ops:
  0.6 62.1 %mega.1 = (f32[1,768]{1,0:T(1,128)}, f32[64,512]{1,0:T(8,128)}, f32[64,128]{1,0:T(8,128)}, f32[256,512]{1,0:T(8,128)}) custom-call(bf16[768,512]{1,0:T(8,128)(2,1)} %hist_hbm.1, s32[2]{0:T(128)} %len_hbm.1, bf16[512,512]{1,0:T(8,128)(2,1)} %w_in_hbm.1, bf16[128,512]{1,0:T(8,128)(2,1)} %w_out_hbm.1, s32[768]{0:T(1024)} %tid_hbm.1, s32[4096]{0:T(1024)} %nid_hbm.1, ...), custom_call_target="tpu_custom_call" | custom-call | tf_op jit(solution)/shard_map/mega/pallas_call | solution.py:852
  62.8 2.0 %finish.1 = (f32[768]{0:T(1024)}, f32[64,512]{1,0:T(8,128)}, f32[64,128]{1,0:T(8,128)}, f32[256,512]{1,0:T(8,128)}) custom-call(f32[1,768]{1,0:T(1,128)} %get-tuple-element.12.loss_in, f32[64,512]{1,0:T(8,128)} %get-tuple-element.13.gwin_in, f32[64,128]{1,0:T(8,128)} %get-tuple-element.14.gwout_in, f32[256,512]{1,0:T(8,128)} %get-tuple-element.15.gtab_in), custom_call_target="tpu_custom_call" | custom-call | tf_op jit(solution)/shard_map/finish/pallas_call | solution.py:876

commit v4 on v3

--- a/solution.py
+++ b/solution.py
@@ -213,10 +213,16 @@
 def columns_to_rows(columns):
     length = columns[0].shape[0]
     place = lax.broadcasted_iota(jnp.int32, (length, LANES), 1)
-    packed = jnp.zeros((length, LANES), f32)
-    for index, column in enumerate(columns):
-        packed = jnp.where(place == index, column, packed)
-    return packed.T[:8]
+    packed = jnp.where(place == 0, columns[0], jnp.where(place == 1, columns[1], 0.0)).T
+    rows = [packed[i : i + 1, j : j + LANES] for i in range(2) for j in range(0, length, LANES)]
+    rows.append(jnp.zeros((8 - len(rows), LANES), f32))
+    return jnp.concatenate(rows, axis=0)
+
+
+def packed_rows(packed, length):
+    count = length // LANES
+    rows = [packed[i : i + 1] for i in range(2 * count)]
+    return jnp.concatenate(rows[:count], axis=1), jnp.concatenate(rows[count:], axis=1)
 
 
 def plan(history, lengths, w_in, w_out, item_table, negative_ids, dp_size, neg_size):
@@ -246,6 +252,7 @@
         s.lw % LANES == 0
         and s.tshare % LANES == 0
         and s.H % LANES == 0
+        and s.H < 4 * LANES
         and s.I % s.CH == 0
         and s.D % LANES == 0
         and s.share % 16 == 0
@@ -256,6 +263,16 @@
         and s.Z == 4
         and s.q % 16 == 0
     )
+
+
+SEND_SLOTS = 40
+
+
+def copy_count(s):
+    gather = 1 + 2 * (s.Y - 1)
+    user = 5 * (s.N - 1) + s.Y + (s.Y - 1) + 2 * gather
+    rows = (s.Z + 1) * (s.X - 1) + s.Z - 1 + s.Z - 1 + s.X - 1
+    return s.U * user + 2 * gather + rows + 2 * (s.Z * (s.X - 1) + s.Z - 1)
 
 
 def scratch_of(s):
@@ -273,10 +290,12 @@
         proj=V((U, H, 4 * lw), bf16),
         scores=V((U, lh, H, H), f32),
         attn=V((U, lh, H, H), bf16),
+        score_grad=V((lh, H, H), bf16),
+        u_t=V((D, U * H), bf16),
         att=V((U, H, lw), f32),
         norm_col=V((U, H, LANES), f32),
-        stat=V((U, N, 8, H), f32),
-        wout_all=V((N, lw, D), bf16),
+        stat=V((U, N, 8, LANES), f32),
+        wout_all=V((2, N, lw // 2, D), bf16),
         mixed_all=V((U, N, H, lw), bf16),
         gate_rows=V((U, N, share, lw), bf16),
         out=V((U, H, D), f32),
@@ -286,7 +305,7 @@
         tid_col=V((U, H, LANES), f32),
         counts=V((I // CH, 1, CH), f32),
         acc=V((U, H, D), f32),
-        zst=V((U, N, 8, H), f32),
+        zst=V((U, N, 8, LANES), f32),
         up=V((U, Y, share, D), bf16),
         r1=V((U, Y, share, D), bf16),
         s2=V((U, Y1, share, D), bf16),
@@ -307,19 +326,24 @@
         zf_rz=V((Z, X, q, tshare), bf16),
         zf_send=V((X1, q, tshare), bf16),
         zf_rx=V((X1, q, tshare), bf16),
-        g_acc=V((D, 5 * lw), f32),
-        g_send=V((Z, X1, wshare, 5 * lw), bf16),
-        g_rx=V((Z, X1, wshare, 5 * lw), bf16),
-        g_zs=V((Z, wshare, 5 * lw), bf16),
-        g_rz=V((Z, wshare, 5 * lw), bf16),
+        gi_acc=V((D, 4 * lw), f32),
+        gi_send=V((Z, X1, wshare, 4 * lw), bf16),
+        gi_rx=V((Z, X1, wshare, 4 * lw), bf16),
+        gi_zs=V((Z, wshare, 4 * lw), bf16),
+        gi_rz=V((Z, wshare, 4 * lw), bf16),
+        go_acc=V((D, lw), f32),
+        go_send=V((Z, X1, wshare, lw), bf16),
+        go_rx=V((Z, X1, wshare, lw), bf16),
+        go_zs=V((Z, wshare, lw), bf16),
+        go_rz=V((Z, wshare, lw), bf16),
         hist=V((U, H, D), bf16),
         w_in=V((D, 4 * lw), bf16),
         tid=V((U * H,), jnp.int32),
         nid=V((s.NB,), jnp.int32),
         length=pltpu.SMEM((U,), jnp.int32),
-        in_sem=pltpu.SemaphoreType.DMA((U + 6,)),
-        ssem=pltpu.SemaphoreType.DMA((192,)),
-        rsem=pltpu.SemaphoreType.DMA((192,)),
+        in_sem=pltpu.SemaphoreType.DMA((U + 7,)),
+        ssem=pltpu.SemaphoreType.DMA((SEND_SLOTS,)),
+        rsem=pltpu.SemaphoreType.DMA((copy_count(s),)),
     )
 
 
@@ -359,34 +383,52 @@
     for peer in everyone:
         pl.semaphore_signal(barrier, inc=1, device_id=peer, device_id_type=MESH)
 
-    sent = []
+    received, flying, free = [], [], list(range(SEND_SLOTS))
 
     def send(src, dst, peer):
-        index = len(sent)
+        index = len(received)
+        slot = free.pop(0)
         copy = pltpu.make_async_remote_copy(
             src_ref=src,
             dst_ref=dst,
-            send_sem=R.ssem.at[index],
+            send_sem=R.ssem.at[slot],
             recv_sem=R.rsem.at[index],
             device_id=peer,
             device_id_type=MESH,
         )
         copy.start()
-        sent.append(copy)
+        received.append(copy)
+        flying.append((slot, copy))
         return copy
 
-    loads = [(w_in_hbm, R.w_in), (w_out_hbm, R.wout_all.at[n])]
+    def settle(keep):
+        while len(flying) > keep:
+            slot, copy = flying.pop(0)
+            copy.wait_send()
+            free.append(slot)
+
+
+    half_rows = lw // 2
+    loads = [(w_in_hbm, R.w_in)]
+    loads += [(w_out_hbm.at[pl.ds(i * half_rows, half_rows)], R.wout_all.at[i, n]) for i in range(2)]
     loads += [(hist_hbm.at[pl.ds(b * H, H)], R.hist.at[b]) for b in range(U)]
     loads += [(item_hbm, R.item_v), (tid_hbm, R.tid), (nid_hbm, R.nid), (len_hbm, R.length)]
     loads = [pltpu.make_async_copy(a, c, R.in_sem.at[i]) for i, (a, c) in enumerate(loads)]
-    w_in_load, w_out_load, hist_loads, item_copy = loads[0], loads[1], loads[2 : 2 + U], loads[2 + U]
+    w_in_load, w_out_loads, hist_loads, item_copy = loads[0], loads[1:3], loads[3 : 3 + U], loads[3 + U]
+    hist_loads[0].start()
     w_in_load.start()
-    for copy in hist_loads:
+    for copy in w_out_loads:
         copy.start()
-    w_out_load.start()
-    for copy in loads[3 + U :]:
+    for copy in hist_loads[1:]:
         copy.start()
-
+    for copy in loads[4 + U :]:
+        copy.start()
+
+    def norm_rows(b):
+        hist_loads[b].wait()
+        R.normed[b] = moment_norm(R.hist[b].astype(f32))[0].astype(bf16)
+
+    norm_rows(0)
     w_in_load.wait()
     w_in = R.w_in[...]
     pieces = []
@@ -396,38 +438,42 @@
             pieces.append(w_in[:, first : first + HEAD])
     R.wperm[...] = jnp.concatenate(pieces, axis=1)
     item_copy.start()
-    loads[5 + U].wait()
+    loads[6 + U].wait()
 
     head_lane = lax.div(lax.broadcasted_iota(jnp.int32, (1, lw), 1), HEAD)
     head_mask = [jnp.where(head_lane == h, 1.0, 0.0).astype(bf16) for h in range(lh)]
 
-    def attn_mask(b):
-        row = lax.broadcasted_iota(jnp.int32, (H, H), 0)
-        col = lax.broadcasted_iota(jnp.int32, (H, H), 1)
+    blocks = H // LANES
+
+    def attn_mask(b, i):
+        width = (i + 1) * LANES
+        row = lax.broadcasted_iota(jnp.int32, (LANES, width), 0) + i * LANES
+        col = lax.broadcasted_iota(jnp.int32, (LANES, width), 1)
         return jnp.where((col <= row) & (row < R.length[b]), 1.0 / H, 0.0)
 
     def part_of(b, part):
         return R.proj[b, :, part * lw : (part + 1) * lw]
 
     def project(b):
-        hist_loads[b].wait()
-        rows = R.hist[b].astype(f32)
-        normed = moment_norm(rows)[0].astype(bf16)
-        R.normed[b] = normed
-        pre = dot_nn(normed, R.wperm[...])
+        pre = dot_nn(R.normed[b], R.wperm[...])
         R.pre[b] = pre
         R.proj[b] = (pre * jax.nn.sigmoid(pre)).astype(bf16)
 
     def attend(b):
         value, query, key = part_of(b, 1), part_of(b, 2), part_of(b, 3)
-        mask = attn_mask(b)
-        total = jnp.zeros((H, lw), f32)
-        for h in range(lh):
-            scores = dot_nt(query * head_mask[h], key)
-            R.scores[b, h] = scores
-            weights = (scores * jax.nn.sigmoid(scores) * mask).astype(bf16)
-            R.attn[b, h] = weights
-            total = total + dot_nn(weights, value * head_mask[h])
+        totals = []
+        for i in range(blocks):
+            rows, width = slice(i * LANES, (i + 1) * LANES), (i + 1) * LANES
+            mask = attn_mask(b, i)
+            total = jnp.zeros((LANES, lw), f32)
+            for h in range(lh):
+                scores = dot_nt(query[rows] * head_mask[h], key[:width])
+                R.scores[b, h, rows, :width] = scores
+                weights = (scores * jax.nn.sigmoid(scores) * mask).astype(bf16)
+                R.attn[b, h, rows, :width] = weights
+                total = total + dot_nn(weights, value[:width] * head_mask[h])
+            totals.append(total)
+        total = jnp.concatenate(totals, axis=0)
         R.att[b] = total
         R.stat[b, n] = columns_to_rows(
             [jnp.sum(total, -1, keepdims=True), jnp.sum(total * total, -1, keepdims=True)]
@@ -447,8 +493,8 @@
         ]
 
     def gather_start(ref):
+        along_y = [send(ref.at[n], ref.at[n], at_neg(turn(y, k, Y) * 2 + core)) for k in range(1, Y)]
         to_partner = send(ref.at[n], ref.at[n], at_neg(partner))
-        along_y = [send(ref.at[n], ref.at[n], at_neg(turn(y, k, Y) * 2 + core)) for k in range(1, Y)]
         return to_partner, along_y
 
     def gather_relay(ref, state):
@@ -465,18 +511,18 @@
             copy.wait_recv()
 
     pl.semaphore_wait(barrier, len(everyone))
-    w_out_load.wait()
-    wout_state = gather_start(R.wout_all)
+    for copy in w_out_loads:
+        copy.wait()
+    wout_states = [gather_start(R.wout_all.at[0])]
     project(0)
     attend(0)
     stat_copies = [send_stats(0)]
-    project(1)
-    attend(1)
     for b in range(1, U):
-        if b > 1:
-            project(b)
-            attend(b)
+        norm_rows(b)
+        project(b)
+        attend(b)
         stat_copies.append(send_stats(b))
+    wout_states.append(gather_start(R.wout_all.at[1]))
 
     item_copy.wait()
     step_rows = CH
@@ -496,8 +542,9 @@
         total = R.stat[b, 0]
         for d in range(1, N):
             total = total + R.stat[b, d]
-        mean = total[0:1] / D
-        scale = lax.rsqrt(total[1:2] / D - mean * mean + epsilon)
+        row_sum, row_square = packed_rows(total, H)
+        mean = row_sum / D
+        scale = lax.rsqrt(row_square / D - mean * mean + epsilon)
         columns = rows_to_columns([mean, scale])
         R.norm_col[b] = columns
         centred = (R.att[b] - columns[:, 0:1]) * columns[:, 1:2]
@@ -506,8 +553,8 @@
         gather_states.append(gather_start(R.mixed_all.at[b]))
 
     mix(0)
-    loads[3 + U].wait()
     loads[4 + U].wait()
+    loads[5 + U].wait()
     slots = R.nid[...].reshape(1, s.NB) - n * I
     high = lax.shift_right_logical(slots, 7)
     low = lax.bitwise_and(slots, LANES - 1)
@@ -539,22 +586,36 @@
         place = lax.broadcasted_iota(jnp.int32, (H, CH), 1) + i * CH
         return ids == place.astype(f32)
 
-    wout_relays = gather_relay(R.wout_all, wout_state)
+    def store_targets(b):
+        for i in range(I // CH):
+            hot = jnp.where(is_target(b, i), 1.0, 0.0).astype(bf16)
+            R.hot[b * H : (b + 1) * H, i * CH : (i + 1) * CH] = hot
+
+    wout_relays = [gather_relay(R.wout_all.at[i], wout_states[i]) for i in range(2)]
     for b in range(U):
         R.normed_t[:, b * H : (b + 1) * H] = R.normed[b].astype(f32).T.astype(bf16)
 
     def prepare_backward(b):
-        mask = attn_mask(b)
-        for h in range(lh):
-            R.scores[b, h] = silu_grad(R.scores[b, h]) * mask
-
+        for i in range(blocks):
+            rows, width = slice(i * LANES, (i + 1) * LANES), (i + 1) * LANES
+            mask = attn_mask(b, i)
+            for h in range(lh):
+                R.scores[b, h, rows, :width] = silu_grad(R.scores[b, h, rows, :width]) * mask
+
+    store_targets(0)
     relays = [gather_relay(R.mixed_all.at[0], gather_states[0])]
-    gather_wait(wout_state, wout_relays)
+    for b in range(1, U):
+        store_targets(b)
+    for state, copies in zip(wout_states, wout_relays):
+        gather_wait(state, copies)
+    def w_out_of(d):
+        return jnp.concatenate([R.wout_all[0, d], R.wout_all[1, d]], axis=0)
+
     z_copies = []
     for b in range(U):
         gather_wait(gather_states[b], relays[b])
         mixed = jnp.concatenate([R.mixed_all[b, d] for d in range(N)], axis=1)
-        w_out_full = R.wout_all[...].reshape(N * lw, D)
+        w_out_full = jnp.concatenate([w_out_of(d) for d in range(N)], axis=0)
         output = R.hist[b].astype(f32) + dot_nn(mixed, w_out_full)
         R.out[b] = output
         unit = normalize_rows(output)[0].astype(bf16)
@@ -572,7 +633,6 @@
             for g in range(groups):
                 partial = partial + terms[:, g * LANES : (g + 1) * LANES]
                 picked = picked + chosen[:, g * LANES : (g + 1) * LANES]
-            R.hot[b * H : (b + 1) * H, cols] = jnp.where(target, 1.0, 0.0).astype(bf16)
             R.exps[b * H : (b + 1) * H, cols] = terms.astype(bf16)
         negative = jnp.sum(partial, -1, keepdims=True)
         positive = jnp.sum(picked, -1, keepdims=True)
@@ -591,17 +651,16 @@
         total = R.zst[b, 0]
         for d in range(1, N):
             total = total + R.zst[b, d]
-        negative, positive = total[0:1], total[1:2]
+        negative, positive = packed_rows(total, H)
         whole = jnp.exp(positive) + negative
         live = lax.broadcasted_iota(jnp.int32, (1, H), 1) < R.length[b]
-        loss_ref[:, b * H : (b + 1) * H] = jnp.where(live, jnp.log(whole) - positive, 0.0)
-        columns = rows_to_columns([jnp.where(live, 1.0 / whole, 0.0), -negative])
-        return columns[:, 0:1], columns[:, 1:2]
-
-    def coefficients(b, factor_col, negative_col):
-        scaled_rows = R.u64[b].astype(f32) * factor_col
-        R.ru_t[:, b * H : (b + 1) * H] = scaled_rows.T.astype(bf16)
-        negative_half = negative_col.astype(bf16)
+        loss = jnp.where(live, jnp.log(whole) - positive, 0.0)
+        loss_ref[b * H : (b + 1) * H] = loss.reshape(H)
+        factor = jnp.where(live, 1.0 / whole, 0.0)
+        columns = rows_to_columns([factor, -negative])
+        at_user = slice(b * H, (b + 1) * H)
+        R.ru_t[:, at_user] = (R.u_t[:, at_user].astype(f32) * factor).astype(bf16)
+        negative_half = columns[:, 1:2].astype(bf16)
 
         def fix(i, carry):
             cols = pl.ds(pl.multiple_of(i * CH, CH), CH)
@@ -609,8 +668,9 @@
             return carry
 
         lax.fori_loop(0, I // CH, fix, 0)
-
-    def unit_send(b, factor_col, negative_col):
+        return columns[:, 0:1]
+
+    def unit_send(b, factor_col):
         total = dot_nn(R.exps[b * H : (b + 1) * H, :], R.item_r[...])
         R.acc[b] = (logit_scale * factor_col) * total
         copies = []
@@ -636,17 +696,19 @@
         return dot_nn(R.ru_t[q:, :], R.exps[:, cols])
 
     z_order = list(range(Z - 1, -1, -1))
-    row_x, g_x = dict(), dict()
+    row_x = dict()
 
     def row_compute(r):
         for kx in range(1, X):
             R.row_send[r, kx - 1] = row_block(flip(z, r) * X + turn(x, kx, X)).astype(bf16)
 
-    def row_start(r):
-        row_x[r] = [
-            send(R.row_send.at[r, kx - 1], R.row_rx.at[r, kx - 1], x_peers[kx - 1])
+    def row_start(r, part=0, parts=1):
+        size = (D - q) // parts
+        some = pl.ds(part * size, size)
+        row_x.setdefault(r, []).extend(
+            send(R.row_send.at[r, kx - 1, some], R.row_rx.at[r, kx - 1, some], x_peers[kx - 1])
             for kx in range(1, X)
-        ]
+        )
 
     def reduce_along_z(r, block, send_ref, recv_ref, slots):
         step = r & -r if r else Z
@@ -659,7 +721,7 @@
             slots[r] = send(send_ref.at[r], recv_ref.at[r], z_peers[step])
         return block
 
-    row_z, g_z, zf_z = dict(), dict(), dict()
+    row_z, zf_z = dict(), dict()
 
     def zfirst_forward(r):
         blocks = []
@@ -669,35 +731,46 @@
             blocks.append(dot_nn(R.ru_t[:q, :], R.exps[:, cols]))
         return reduce_along_z(r, jnp.stack(blocks), R.zf_zs, R.zf_rz, zf_z)
 
+    def turn_rows(b):
+        R.u_t[:, b * H : (b + 1) * H] = R.u64[b].astype(f32).T.astype(bf16)
+
+    settle(len(z_copies) * (N - 1))
+    for b in range(U - 1):
+        turn_rows(b)
+        unit_send(b, partition(b))
+        if b > 0:
+            unit_relay(b - 1)
+    turn_rows(U - 1)
+    factor_col = partition(U - 1)
+    for r in z_order:
+        if r % 2 == 1:
+            zfirst_forward(r)
+    if U > 1:
+        unit_relay(U - 2)
+    row_compute(z_order[0])
+    row_start(z_order[0])
+    unit_send(U - 1, factor_col)
+    row_compute(z_order[1])
+    row_start(z_order[1])
+    unit_relay(U - 1)
     for b in range(U):
-        if b == U - 1:
-            columns = partition(b)
-            coefficients(b, *columns)
-            for r in z_order:
-                if r % 2 == 1:
-                    zfirst_forward(r)
-            row_compute(z_order[0])
-            row_start(z_order[0])
-            if b > 0:
-                unit_relay(b - 1)
-            unit_send(b, *columns)
-        else:
-            columns = partition(b)
-            coefficients(b, *columns)
-            unit_send(b, *columns)
-            if b > 0:
-                unit_relay(b - 1)
-    row_compute(z_order[1])
-    unit_relay(U - 1)
+        prepare_backward(b)
     for r in z_order[2:]:
         row_compute(r)
-    for b in range(U):
-        prepare_backward(b)
     for r in z_order:
         R.row_own[r] = row_block(flip(z, r) * X + x)
-    row_start(z_order[1])
     zfirst_forward(2)
-
+    row_start(z_order[2])
+
+    def row_forward(r):
+        block = R.row_own[r]
+        for copy in row_x[r]:
+            copy.wait_recv()
+        for kx in range(1, X):
+            block = block + R.row_rx[r, kx - 1].astype(f32)
+        return reduce_along_z(r, block, R.row_zs, R.row_rz, row_z)
+
+    settle(8)
     for copies in gate_copies:
         for copy in copies:
             copy.wait_recv()
@@ -714,7 +787,7 @@
         sum_g = jnp.zeros((share, 1), f32)
         sum_gc = jnp.zeros((share, 1), f32)
         for d in range(N):
-            mixed_grad = dot_nt(half, R.wout_all[d])
+            mixed_grad = dot_nt(half, w_out_of(d))
             R.mg_send[b, d] = mixed_grad.astype(bf16)
             sum_g = sum_g + jnp.sum(mixed_grad * R.gate_rows[b, d].astype(f32), -1, keepdims=True)
             mixed = R.mixed_all[b, d, share_rows(n), :].astype(f32)
@@ -732,16 +805,11 @@
             copies.append(send(R.mg_send.at[b, p], R.mg_recv.at[b, n], at_neg(p)))
             copies.append(send(R.bs_send.at[b], R.bs_recv.at[b, n], at_neg(p)))
         mg_copies.append(copies)
+        if b == 0:
+            row_forward(z_order[0])
+    for b in range(U):
         og_states.append(gather_start(R.og_all.at[b]))
-    row_start(z_order[2])
-
-
-    def row_forward(r):
-        block = R.row_own[r]
-        for kx in range(1, X):
-            row_x[r][kx - 1].wait_recv()
-            block = block + R.row_rx[r, kx - 1].astype(f32)
-        return reduce_along_z(r, block, R.row_zs, R.row_rz, row_z)
+
 
     def backward(b):
         for copy in mg_copies[b]:
@@ -759,67 +827,95 @@
         scale = R.norm_col[b][:, 1:2]
         grad = mixed_grad * gate
         attended_grad = (scale * (grad - sums[:, 0:1] - centred * sums[:, 1:2])).astype(bf16)
-        value_grad = jnp.zeros((H, lw), f32)
-        query_grad = jnp.zeros((H, lw), f32)
-        key_grad = jnp.zeros((H, lw), f32)
-        for h in range(lh):
-            own = attended_grad * head_mask[h]
-            value_grad = value_grad + dot_tn(R.attn[b, h], own)
-            score_grad = (dot_nt(own, value) * R.scores[b, h]).astype(bf16)
-            query_grad = query_grad + dot_nn(score_grad, key * head_mask[h])
-            key_grad = key_grad + dot_tn(score_grad, query * head_mask[h])
+        query_grads, key_grads, value_grads = [], [], []
+        for i in range(blocks):
+            rows, width = slice(i * LANES, (i + 1) * LANES), (i + 1) * LANES
+            query_grad = jnp.zeros((LANES, lw), f32)
+            for h in range(lh):
+                weight_grad = dot_nt(attended_grad[rows] * head_mask[h], value[:width])
+                score_grad = (weight_grad * R.scores[b, h, rows, :width]).astype(bf16)
+                R.score_grad[h, rows, :width] = score_grad
+                query_grad = query_grad + dot_nn(score_grad, key[:width] * head_mask[h])
+            query_grads.append(query_grad)
+        for j in range(blocks):
+            first, cols = j * LANES, slice(j * LANES, (j + 1) * LANES)
+            key_grad = jnp.zeros((LANES, lw), f32)
+            value_grad = jnp.zeros((LANES, lw), f32)
+            for h in range(lh):
+                own = attended_grad[first:] * head_mask[h]
+                value_grad = value_grad + dot_tn(R.attn[b, h, first:, cols], own)
+                key_grad = key_grad + dot_tn(R.score_grad[h, first:, cols], query[first:] * head_mask[h])
+            key_grads.append(key_grad)
+            value_grads.append(value_grad)
+        value_grad = jnp.concatenate(value_grads, axis=0)
+        query_grad = jnp.concatenate(query_grads, axis=0)
+        key_grad = jnp.concatenate(key_grads, axis=0)
         project_grad = jnp.concatenate([mixed_grad * centred, value_grad, query_grad, key_grad], axis=1)
         pre_grad = (project_grad * silu_grad(R.pre[b])).astype(bf16)
         part = dot_nn(R.normed_t[:, b * H : (b + 1) * H], pre_grad)
         if b == 0:
-            R.g_acc[:, 0 : 4 * lw] = part
+            R.gi_acc[...] = part
         else:
-            R.g_acc[:, 0 : 4 * lw] += part
-
-    row_forward(z_order[0])
+            R.gi_acc[...] += part
+
     backward(0)
-    og_relays.append(gather_relay(R.og_all.at[0], og_states[0]))
+    row_start(0, 0, 2)
     for b in range(1, U):
         backward(b)
-    for b in range(1, U):
+
+    w_order = [r for r in z_order if r % 2 == 1] + [r for r in z_order if r % 2 == 0]
+    def weight_start(acc, send_ref, recv_ref):
+        copies = dict()
+        for r in w_order:
+            copies[r] = []
+            for kx in range(1, X):
+                first = (flip(z, r) * X + turn(x, kx, X)) * wshare
+                send_ref[r, kx - 1] = acc[pl.ds(pl.multiple_of(first, 8), wshare), :].astype(bf16)
+                copies[r].append(
+                    send(send_ref.at[r, kx - 1], recv_ref.at[r, kx - 1], x_peers[kx - 1])
+                )
+        return copies
+
+    def weight_forward(r, copies, slots, acc, recv_ref, zs, rz):
+        first = (flip(z, r) * X + x) * wshare
+        block = acc[pl.ds(pl.multiple_of(first, 8), wshare), :]
+        for kx in range(1, X):
+            copies[r][kx - 1].wait_recv()
+            block = block + recv_ref[r, kx - 1].astype(f32)
+        return reduce_along_z(r, block, zs, rz, slots)
+
+    settle(8)
+    gi_x = weight_start(R.gi_acc, R.gi_send, R.gi_rx)
+    row_forward(z_order[1])
+    row_forward(z_order[2])
+    for b in range(U):
         og_relays.append(gather_relay(R.og_all.at[b], og_states[b]))
+    grad_out = jnp.zeros((lw, D), f32)
+    for b in range(U):
+        gather_wait(og_states[b], og_relays[b])
+        grad_out = grad_out + dot_tn(R.mixed_all[b, n], R.og_all[b].reshape(H, D))
+    R.go_acc[...] = grad_out.T
+    go_x = weight_start(R.go_acc, R.go_send, R.go_rx)
     R.zf_own[...] = zfirst_forward(0)
     zf_x = []
     for kx in range(1, X):
         R.zf_send[kx - 1] = R.zf_own[kx].astype(bf16)
         zf_x.append(send(R.zf_send.at[kx - 1], R.zf_rx.at[kx - 1], x_peers[kx - 1]))
-    row_forward(z_order[1])
-    grad_out = jnp.zeros((lw, D), f32)
-    for b in range(U):
-        gather_wait(og_states[b], og_relays[b])
-        grad_out = grad_out + dot_tn(R.mixed_all[b, n], R.og_all[b].reshape(H, D))
-    R.g_acc[:, 4 * lw : 5 * lw] = grad_out.T
-
-    def g_rows(index):
-        return R.g_acc[pl.ds(pl.multiple_of(index * wshare, 8), wshare), :]
-
-    for r in z_order:
-        for kx in range(1, X):
-            R.g_send[r, kx - 1] = g_rows(flip(z, r) * X + turn(x, kx, X)).astype(bf16)
-        g_x[r] = [
-            send(R.g_send.at[r, kx - 1], R.g_rx.at[r, kx - 1], x_peers[kx - 1])
-            for kx in range(1, X)
-        ]
-    row_start(z_order[3])
-    row_forward(z_order[2])
-    for r in z_order:
-        block = g_rows(flip(z, r) * X + x)
-        for kx in range(1, X):
-            g_x[r][kx - 1].wait_recv()
-            block = block + R.g_rx[r, kx - 1].astype(f32)
-        own_g = reduce_along_z(r, block, R.g_zs, R.g_rz, g_z)
+    row_start(0, 1, 2)
+    gi_z, go_z = dict(), dict()
+    for r in w_order[:-1]:
+        weight_forward(r, gi_x, gi_z, R.gi_acc, R.gi_rx, R.gi_zs, R.gi_rz)
+    for r in w_order[:-1]:
+        weight_forward(r, go_x, go_z, R.go_acc, R.go_rx, R.go_zs, R.go_rz)
+    own_in = weight_forward(0, gi_x, gi_z, R.gi_acc, R.gi_rx, R.gi_zs, R.gi_rz)
+    own_out = weight_forward(0, go_x, go_z, R.go_acc, R.go_rx, R.go_zs, R.go_rz)
     pieces = []
     for h in range(lh):
         for part in range(4):
             first = part * lw + h * HEAD
-            pieces.append(own_g[:, first : first + HEAD])
+            pieces.append(own_in[:, first : first + HEAD])
     gwin_ref[...] = jnp.concatenate(pieces, axis=1)
-    gwout_ref[...] = own_g[:, 4 * lw : 5 * lw]
+    gwout_ref[...] = own_out
     first_part = R.zf_own[0]
     for kx in range(1, X):
         zf_x[kx - 1].wait_recv()
@@ -828,15 +924,20 @@
     own_items = R.item_v[pl.ds(pl.multiple_of(me_dp * tshare, 16), tshare), :].astype(f32)
     unit, inverse = normalize_rows(own_items)
     gtab_ref[...] = project_rows(row_total.T, unit, inverse)
-    for copy in sent:
-        copy.wait_send()
-
-
-def finish(loss_in, gwin_in, gwout_in, gtab_in, loss_ref, gwin_ref, gwout_ref, gtab_ref):
-    loss_ref[...] = loss_in[...].reshape(loss_ref.shape)
-    gwin_ref[...] = gwin_in[...]
-    gwout_ref[...] = gwout_in[...]
-    gtab_ref[...] = gtab_in[...]
+    settle(0)
+    assert len(received) == copy_count(s)
+
+
+def finish(*refs):
+    half = len(refs) // 2
+    sem = refs[-1]
+    copies = [
+        pltpu.make_async_copy(refs[i], refs[half + i], sem.at[i]) for i in range(half)
+    ]
+    for copy in copies:
+        copy.start()
+    for copy in copies:
+        copy.wait()
 
 
 def on_device(dp_size, neg_size, history, lengths, w_in, w_out, target_ids, negative_ids, item_table):
@@ -852,10 +953,10 @@
     loss, grad_in, grad_out, grad_table = pl.pallas_call(
         functools.partial(mega, s, tuple(scratch)),
         out_shape=(
-            jax.ShapeDtypeStruct((1, U * H), f32),
-            jax.ShapeDtypeStruct((s.wshare, 4 * lw), f32),
-            jax.ShapeDtypeStruct((s.wshare, lw), f32),
-            jax.ShapeDtypeStruct((s.tshare, D), f32),
+            pltpu.VMEM((U * H,), f32),
+            pltpu.VMEM((s.wshare, 4 * lw), f32),
+            pltpu.VMEM((s.wshare, lw), f32),
+            pltpu.VMEM((s.tshare, D), f32),
         ),
         in_specs=[hbm] * 7,
         out_specs=(vmem, vmem, vmem, vmem),
@@ -882,9 +983,10 @@
             jax.ShapeDtypeStruct((s.tshare, D), f32),
         ),
         in_specs=[vmem] * 4,
-        out_specs=(vmem,) * 4,
+        out_specs=(hbm,) * 4,
+        scratch_shapes=[pltpu.SemaphoreType.DMA((4,))],
         name="finish",
-    )(loss, grad_in, grad_out, grad_table)
+    )(*(pltpu.with_memory_space_constraint(v, pltpu.VMEM) for v in (loss, grad_in, grad_out, grad_table)))
     return (loss, grad_in, grad_out.T, grad_table)
 
 

time: 64.9 us -> 62 us (0.955)
  Pallas kernels: 64.1 us -> 61.1 us
    pallas_call x1, Pallas kernels: 62.1 us -> 60.2 us  [on_device(): pl.pallas_call(functools.partial(mega, s, tuple(scratch)), out_shape=(plt...]
    pallas_call x1, Pallas kernels: 2 us -> 0.89 us  [on_device(): pl.pallas_call(finish, out_shape=(jax.ShapeDtypeStruct((U * H,), f32), ja...]
where the time goes in v4:
time: 62 us; the launch traced here: 61.9 us
  Pallas kernels  61.1 us (99%)
  between operations  0.8 us (1%)
    pallas_call x1, Pallas kernels, on_device(): pl.pallas_call(functools.partial(mega, s, tuple(scratch)), out_shape=(plt...  60.2 us

profile of v4, /device:TPU:0, one launch (start us, length us, event | category | flops | bytes accessed | tf_op | source)
XLA Modules:
  0.0 61.9 jit_solution(9452387396383294969)
XLA Ops:
  0.6 60.2 %mega.1 = (f32[768]{0:T(1024)S(1)}, f32[64,512]{1,0:T(8,128)S(1)}, f32[64,128]{1,0:T(8,128)S(1)}, f32[256,512]{1,0:T(8,128)S(1)}) custom-call(bf16[768,512]{1,0:T(8,128)(2,1)} %hist_hbm.1, s32[2]{0:T(128)} %len_hbm.1, bf16[512,512]{1,0:T(8,128)(2,1)} %w_in_hbm.1, bf16[128,512]{1,0:T(8,128)(2,1)} %w_out_hbm.1, s32[768]{0:T(1024)} %tid_hbm.1, s32[4096]{0:T(1024)} %nid_hbm.1, ...), custom_call_target="tpu_custom_call" | custom-call | tf_op jit(solution)/shard_map/mega/pallas_call | solution.py:953
  60.8 0.9 %finish.1 = (f32[768]{0:T(1024)}, f32[64,512]{1,0:T(8,128)}, f32[64,128]{1,0:T(8,128)}, f32[256,512]{1,0:T(8,128)}) custom-call(f32[768]{0:T(1024)S(1)} %get-tuple-element.12.refs_0_, f32[64,512]{1,0:T(8,128)S(1)} %get-tuple-element.13.refs_1_, f32[64,128]{1,0:T(8,128)S(1)} %get-tuple-element.14.refs_2_, f32[256,512]{1,0:T(8,128)S(1)} %get-tuple-element.15.refs_3_), custom_call_target="tpu_custom_call" | custom-call | tf_op jit(solution)/shard_map/finish/pallas_call | solution.py:977

commit v5 on v4

--- a/solution.py
+++ b/solution.py
@@ -265,13 +265,13 @@
     )
 
 
-SEND_SLOTS = 40
+SEND_SLOTS = 58
 
 
 def copy_count(s):
     gather = 1 + 2 * (s.Y - 1)
     user = 5 * (s.N - 1) + s.Y + (s.Y - 1) + 2 * gather
-    rows = (s.Z + 1) * (s.X - 1) + s.Z - 1 + s.Z - 1 + s.X - 1
+    rows = (s.Z + 2) * (s.X - 1) + s.Z + s.Z - 1 + s.X - 1
     return s.U * user + 2 * gather + rows + 2 * (s.Z * (s.X - 1) + s.Z - 1)
 
 
@@ -376,7 +376,7 @@
         return index
 
     levels = [1 << k for k in range(Z.bit_length() - 1)]
-    z_peers = {bit: (flip(z, bit) * X + x, n) for bit in levels}
+    z_peers = {r: (flip(z, r) * X + x, n) for r in range(1, Z)}
     everyone = [at_neg(p) for p in neg_peers] + x_peers + list(z_peers.values())
 
     barrier = pltpu.get_barrier_semaphore()
@@ -714,11 +714,12 @@
         step = r & -r if r else Z
         for bit in levels:
             if bit < step:
-                slots[r ^ bit].wait_recv()
+                for copy in slots[r ^ bit]:
+                    copy.wait_recv()
                 block = block + recv_ref[r ^ bit].astype(f32)
         if r:
             send_ref[r] = block.astype(bf16)
-            slots[r] = send(send_ref.at[r], recv_ref.at[r], z_peers[step])
+            slots[r] = [send(send_ref.at[r], recv_ref.at[r], z_peers[step])]
         return block
 
     row_z, zf_z = dict(), dict()
@@ -748,7 +749,8 @@
     if U > 1:
         unit_relay(U - 2)
     row_compute(z_order[0])
-    row_start(z_order[0])
+    for part in range(2):
+        row_start(z_order[0], part, 2)
     unit_send(U - 1, factor_col)
     row_compute(z_order[1])
     row_start(z_order[1])
@@ -759,8 +761,17 @@
         row_compute(r)
     for r in z_order:
         R.row_own[r] = row_block(flip(z, r) * X + x)
-    zfirst_forward(2)
-    row_start(z_order[2])
+    def row_forward_part(r, part, parts):
+        size = (D - q) // parts
+        some = pl.ds(part * size, size)
+        block = R.row_own[r, some]
+        for kx in range(1, X):
+            row_x[r][part * (X - 1) + kx - 1].wait_recv()
+            block = block + R.row_rx[r, kx - 1, some].astype(f32)
+        R.row_zs[r, some] = block.astype(bf16)
+        row_z.setdefault(r, []).append(
+            send(R.row_zs.at[r, some], R.row_rz.at[r, some], z_peers[1])
+        )
 
     def row_forward(r):
         block = R.row_own[r]
@@ -770,7 +781,10 @@
             block = block + R.row_rx[r, kx - 1].astype(f32)
         return reduce_along_z(r, block, R.row_zs, R.row_rz, row_z)
 
-    settle(8)
+    row_forward_part(z_order[0], 0, 2)
+    zfirst_forward(2)
+    row_start(z_order[2])
+
     for copies in gate_copies:
         for copy in copies:
             copy.wait_recv()
@@ -806,7 +820,7 @@
             copies.append(send(R.bs_send.at[b], R.bs_recv.at[b, n], at_neg(p)))
         mg_copies.append(copies)
         if b == 0:
-            row_forward(z_order[0])
+            row_forward_part(z_order[0], 1, 2)
     for b in range(U):
         og_states.append(gather_start(R.og_all.at[b]))
 
@@ -860,10 +874,11 @@
 
     backward(0)
     row_start(0, 0, 2)
+    row_forward(z_order[1])
     for b in range(1, U):
         backward(b)
 
-    w_order = [r for r in z_order if r % 2 == 1] + [r for r in z_order if r % 2 == 0]
+    w_order = z_order
     def weight_start(acc, send_ref, recv_ref):
         copies = dict()
         for r in w_order:
@@ -882,11 +897,16 @@
         for kx in range(1, X):
             copies[r][kx - 1].wait_recv()
             block = block + recv_ref[r, kx - 1].astype(f32)
-        return reduce_along_z(r, block, zs, rz, slots)
-
-    settle(8)
+        if r:
+            zs[r] = block.astype(bf16)
+            slots[r] = send(zs.at[r], rz.at[r], z_peers[r])
+            return None
+        for other in range(1, Z):
+            slots[other].wait_recv()
+            block = block + rz[other].astype(f32)
+        return block
+
     gi_x = weight_start(R.gi_acc, R.gi_send, R.gi_rx)
-    row_forward(z_order[1])
     row_forward(z_order[2])
     for b in range(U):
         og_relays.append(gather_relay(R.og_all.at[b], og_states[b]))

time: 62 us -> 58.9 us (0.950)
  Pallas kernels: 61.1 us -> 58 us
    pallas_call x1, Pallas kernels: 60.2 us -> 57.1 us  [on_device(): pl.pallas_call(functools.partial(mega, s, tuple(scratch)), out_shape=(plt...]
where the time goes in v5:
time: 58.9 us; the launch traced here: 58.8 us
  Pallas kernels  58 us (98%)
  between operations  0.8 us (1%)
    pallas_call x1, Pallas kernels, on_device(): pl.pallas_call(functools.partial(mega, s, tuple(scratch)), out_shape=(plt...  57.1 us

profile of v5, /device:TPU:0, one launch (start us, length us, event | category | flops | bytes accessed | tf_op | source)
XLA Modules:
  0.0 58.8 jit_solution(13794952542430007533)
XLA Ops:
  0.6 57.1 %mega.1 = (f32[768]{0:T(1024)S(1)}, f32[64,512]{1,0:T(8,128)S(1)}, f32[64,128]{1,0:T(8,128)S(1)}, f32[256,512]{1,0:T(8,128)S(1)}) custom-call(bf16[768,512]{1,0:T(8,128)(2,1)} %hist_hbm.1, s32[2]{0:T(128)} %len_hbm.1, bf16[512,512]{1,0:T(8,128)(2,1)} %w_in_hbm.1, bf16[128,512]{1,0:T(8,128)(2,1)} %w_out_hbm.1, s32[768]{0:T(1024)} %tid_hbm.1, s32[4096]{0:T(1024)} %nid_hbm.1, ...), custom_call_target="tpu_custom_call" | custom-call | tf_op jit(solution)/shard_map/mega/pallas_call | solution.py:973
  57.7 0.9 %finish.1 = (f32[768]{0:T(1024)}, f32[64,512]{1,0:T(8,128)}, f32[64,128]{1,0:T(8,128)}, f32[256,512]{1,0:T(8,128)}) custom-call(f32[768]{0:T(1024)S(1)} %get-tuple-element.12.refs_0_, f32[64,512]{1,0:T(8,128)S(1)} %get-tuple-element.13.refs_1_, f32[64,128]{1,0:T(8,128)S(1)} %get-tuple-element.14.refs_2_, f32[256,512]{1,0:T(8,128)S(1)} %get-tuple-element.15.refs_3_), custom_call_target="tpu_custom_call" | custom-call | tf_op jit(solution)/shard_map/finish/pallas_call | solution.py:997

commit v6 on v5

--- a/solution.py
+++ b/solution.py
@@ -271,7 +271,7 @@
 def copy_count(s):
     gather = 1 + 2 * (s.Y - 1)
     user = 5 * (s.N - 1) + s.Y + (s.Y - 1) + 2 * gather
-    rows = (s.Z + 2) * (s.X - 1) + s.Z + s.Z - 1 + s.X - 1
+    rows = (s.Z + 1) * (s.X - 1) + s.Z + s.Z - 1 + s.X - 1
     return s.U * user + 2 * gather + rows + 2 * (s.Z * (s.X - 1) + s.Z - 1)
 
 
@@ -873,7 +873,6 @@
             R.gi_acc[...] += part
 
     backward(0)
-    row_start(0, 0, 2)
     row_forward(z_order[1])
     for b in range(1, U):
         backward(b)
@@ -921,7 +920,7 @@
     for kx in range(1, X):
         R.zf_send[kx - 1] = R.zf_own[kx].astype(bf16)
         zf_x.append(send(R.zf_send.at[kx - 1], R.zf_rx.at[kx - 1], x_peers[kx - 1]))
-    row_start(0, 1, 2)
+    row_start(0)
     gi_z, go_z = dict(), dict()
     for r in w_order[:-1]:
         weight_forward(r, gi_x, gi_z, R.gi_acc, R.gi_rx, R.gi_zs, R.gi_rz)

time: 58.9 us -> 58.9 us (level)
  no operation moved by 1% of the time
where the time goes in v6:
time: 58.9 us; the launch traced here: 58.7 us
  Pallas kernels  57.9 us (98%)
  between operations  0.8 us (1%)
    pallas_call x1, Pallas kernels, on_device(): pl.pallas_call(functools.partial(mega, s, tuple(scratch)), out_shape=(plt...  57.1 us

profile of v6, /device:TPU:0, one launch (start us, length us, event | category | flops | bytes accessed | tf_op | source)
XLA Modules:
  0.0 58.7 jit_solution(18018730793718422068)
XLA Ops:
  0.6 57.1 %mega.1 = (f32[768]{0:T(1024)S(1)}, f32[64,512]{1,0:T(8,128)S(1)}, f32[64,128]{1,0:T(8,128)S(1)}, f32[256,512]{1,0:T(8,128)S(1)}) custom-call(bf16[768,512]{1,0:T(8,128)(2,1)} %hist_hbm.1, s32[2]{0:T(128)} %len_hbm.1, bf16[512,512]{1,0:T(8,128)(2,1)} %w_in_hbm.1, bf16[128,512]{1,0:T(8,128)(2,1)} %w_out_hbm.1, s32[768]{0:T(1024)} %tid_hbm.1, s32[4096]{0:T(1024)} %nid_hbm.1, ...), custom_call_target="tpu_custom_call" | custom-call | tf_op jit(solution)/shard_map/mega/pallas_call | solution.py:972
  57.7 0.9 %finish.1 = (f32[768]{0:T(1024)}, f32[64,512]{1,0:T(8,128)}, f32[64,128]{1,0:T(8,128)}, f32[256,512]{1,0:T(8,128)}) custom-call(f32[768]{0:T(1024)S(1)} %get-tuple-element.12.refs_0_, f32[64,512]{1,0:T(8,128)S(1)} %get-tuple-element.13.refs_1_, f32[64,128]{1,0:T(8,128)S(1)} %get-tuple-element.14.refs_2_, f32[256,512]{1,0:T(8,128)S(1)} %get-tuple-element.15.refs_3_), custom_call_target="tpu_custom_call" | custom-call | tf_op jit(solution)/shard_map/finish/pallas_call | solution.py:996
